TPU v7x, 32 devices: a whole 2x2x4 slice. The times are simulated.
32 devices in a mesh: groups: 2 (over y), store: 16 (over z, x, core).
Axes of the slice: x: 2, y: 2, z: 4, core: 2. Of those that a mesh axis runs over, the one named last changes fastest.
Arguments:
- queries: bfloat16 [2, 32, 8192], P(None, ('groups', 'store')), parts along dimension 1, may hold values from -6 to 206
- new_keys: bfloat16 [2, 32, 1024], P(None, ('groups', 'store')), parts along dimension 1, may hold values from -6 to 12.5
- incoming_values: bfloat16 [2, 32, 1024], P(None, ('groups', 'store')), parts along dimension 1, may hold values from -6 to 6
- key_left: bfloat16 [32, 4096, 160], P(('groups', 'store')), parts along dimension 0, may hold values from -12 to 12
- right_key_factor: bfloat16 [32, 160, 1024], P(('groups', 'store')), parts along dimension 0, may hold values from -0.5 to 0.5
- value_tile_store: bfloat16 [131072, 1024], P(('groups', 'store')), parts along dimension 0, may hold values from -6 to 6
- slot_map: int32 [32, 8, 512], P(('groups', 'store')), parts along dimension 0, may hold values from 0 to 65535, as said below
- chosen: int32 [2, 32, 8, 64], P(None, ('groups', 'store')), parts along dimension 1, may hold values from 0 to 511, as said below
- lengths: int32 [32], P(('groups', 'store')), parts along dimension 0, may hold values from 1024 to 4096
Outputs:
- attended: bfloat16 [2, 32, 8192], P(None, ('groups', 'store')), parts along dimension 1
There are 2 independent parts, one for each index of `groups`. A program takes and returns all parts, laid end to end along the dimension named above; each array names one. Nothing has to cross between parts.
Inputs may be any that keep to these rules, and one draw needn't show every extreme that they name: `slot_map`: the entries are distinct; pool rows r * 4096 to (r+1) * 4096 - 1 stand on index r of store. `chosen`: the 64 blocks of one step, request and key head are distinct; at most 8 of them have their slot_map row on one index of store, and in every step some index of store holds exactly 8 of them for every request and key head.
All inputs are finite; a program needn't handle non-finite values.
Results may differ from a plain program's by a relative error of at most 0.005.
The roundings to bfloat16 on the way count: a program that leaves them out, or rounds other values in their place, can miss the bound.
Values may be sent and summed in bfloat16 or wider, within the bound.
A program may use at most 64 MiB of HBM per device.

v0:
```python
import functools

import jax
import jax.numpy as jnp
import numpy as np
from jax import lax
from jax.experimental import pallas as pl
from jax.experimental.pallas import tpu as pltpu
from jax.sharding import PartitionSpec as P

KEY_VALUE_HEADS = 8
HEAD_SIZE = 128
BLOCK_TOKENS = 8


ROPE_BASE = 500000.0


def apply_rotary(tensor, token_positions):
    half_dim = tensor.shape[-1] // 2
    inverse = ROPE_BASE ** (-(jnp.arange(half_dim, dtype=jnp.float32) * 2.0 / tensor.shape[-1]))
    angles = jnp.asarray(token_positions).astype(jnp.float32)[..., None] * inverse
    cosine = jnp.cos(angles)
    sine_vals = jnp.sin(angles)
    first_half = tensor[..., :half_dim]
    second_half = tensor[..., half_dim:]
    return jnp.concatenate(
        [
            first_half * cosine - second_half * sine_vals,
            second_half * cosine + first_half * sine_vals,
        ],
        -1,
    )


def fetch_tiles(requests, value_tile_store):
    tile_row_index = jnp.take(
        value_tile_store,
        lax.all_to_all(requests, "store", split_axis=0, concat_axis=0, tiled=True),
        axis=0,
    )
    return lax.all_to_all(tile_row_index, "store", split_axis=0, concat_axis=0, tiled=True)


def build_requests(flat_idx, inside, total):
    buffer = jnp.zeros((total,), jnp.int32)
    return buffer.at[flat_idx.reshape(-1)].set(inside.reshape(-1))


def attend_row(
    query_full,
    incoming_keys_full,
    incoming_values_full,
    left_rows,
    right_factor_rows,
    block_numbers,
    tile_row_index,
    length,
    step_index,
):
    query_group_size = query_full.shape[-1] // HEAD_SIZE // KEY_VALUE_HEADS
    every_head = query_group_size * KEY_VALUE_HEADS
    selected_count = block_numbers.shape[1]
    score_scale = HEAD_SIZE ** (-0.5)
    right_factor_heads = right_factor_rows.reshape(
        right_factor_rows.shape[0], KEY_VALUE_HEADS, HEAD_SIZE
    )
    token_positions = (
        block_numbers[:, :, None] * BLOCK_TOKENS + jnp.arange(BLOCK_TOKENS, dtype=jnp.int32)
    ).reshape(KEY_VALUE_HEADS, selected_count * BLOCK_TOKENS)
    picked = left_rows[token_positions]
    raw_keys = jnp.einsum(
        "htr,rhd->htd", picked, right_factor_heads, preferred_element_type=jnp.float32
    )
    cache_keys = apply_rotary(raw_keys, token_positions).astype(jnp.bfloat16)
    rotated_query = apply_rotary(
        query_full[step_index].reshape(every_head, HEAD_SIZE).astype(jnp.float32),
        length + step_index,
    ).astype(jnp.bfloat16)
    current_position = (length + jnp.arange(step_index + 1, dtype=jnp.int32))[:, None]
    current_keys = apply_rotary(
        incoming_keys_full[: step_index + 1]
        .reshape(step_index + 1, KEY_VALUE_HEADS, HEAD_SIZE)
        .astype(jnp.float32),
        current_position,
    ).astype(jnp.bfloat16)
    current_keys = jnp.transpose(current_keys, (1, 0, 2))
    current_values = jnp.transpose(
        incoming_values_full[: step_index + 1].reshape(step_index + 1, KEY_VALUE_HEADS, HEAD_SIZE),
        (1, 0, 2),
    )
    local_values = tile_row_index.reshape(KEY_VALUE_HEADS, selected_count * BLOCK_TOKENS, HEAD_SIZE)
    grouped_queries = rotated_query.reshape(KEY_VALUE_HEADS, query_group_size, HEAD_SIZE)
    cache_scores = (
        jnp.einsum("hgd,htd->hgt", grouped_queries, cache_keys, preferred_element_type=jnp.float32)
        * score_scale
    )
    inside_len = token_positions < length
    cache_scores = jnp.where(inside_len[:, None, :], cache_scores, -jnp.inf)
    fresh_scores = (
        jnp.einsum(
            "hgd,hnd->hgn", grouped_queries, current_keys, preferred_element_type=jnp.float32
        )
        * score_scale
    )
    highest = jnp.maximum(
        jnp.max(cache_scores, -1, keepdims=True), jnp.max(fresh_scores, -1, keepdims=True)
    )
    cache_exp = jnp.exp(cache_scores - highest)
    fresh_exp = jnp.exp(fresh_scores - highest)
    denominator = jnp.sum(cache_exp, -1, keepdims=True) + jnp.sum(fresh_exp, -1, keepdims=True)
    cache_weight = (cache_exp / denominator).astype(jnp.bfloat16)
    fresh_weight = (fresh_exp / denominator).astype(jnp.bfloat16)
    attended = jnp.einsum(
        "hgt,htd->hgd", cache_weight, local_values, preferred_element_type=jnp.float32
    )
    attended = attended + jnp.einsum(
        "hgn,hnd->hgd", fresh_weight, current_values, preferred_element_type=jnp.float32
    )
    return attended.reshape(every_head * HEAD_SIZE).astype(jnp.bfloat16)


def per_device(
    queries,
    new_keys,
    incoming_values,
    key_left,
    right_key_factor,
    value_tile_store,
    slot_map,
    chosen,
    lengths,
):
    nstore = lax.axis_size("store")
    local_rows = key_left.shape[0]
    nchunk = slot_map.shape[2]
    step_count = chosen.shape[0]
    selected_count = chosen.shape[3]
    keeper_share = max(1, nchunk // nstore // 4)
    tile_limit = local_rows * KEY_VALUE_HEADS * keeper_share
    pool_here = value_tile_store.shape[0]
    slot_numbers = jnp.take_along_axis(
        jnp.broadcast_to(slot_map[None], (step_count,) + slot_map.shape), chosen, axis=3
    )
    tile_keeper = slot_numbers // pool_here
    inside = slot_numbers % pool_here
    matched = tile_keeper[..., :, None] == tile_keeper[..., None, :]
    earlier = jnp.arange(selected_count)[None, :] < jnp.arange(selected_count)[:, None]
    order_in = jnp.sum(jnp.logical_and(matched, earlier), -1)
    row_head = (
        jnp.arange(local_rows, dtype=jnp.int32)[:, None, None] * KEY_VALUE_HEADS
        + jnp.arange(KEY_VALUE_HEADS, dtype=jnp.int32)[None, :, None]
    )
    position = row_head * keeper_share + order_in
    tiles_all = []
    slot_span = step_count * tile_limit
    flat_idx = (
        tile_keeper * slot_span
        + jnp.arange(step_count, dtype=jnp.int32)[:, None, None, None] * tile_limit
        + position
    )
    requests = build_requests(flat_idx, inside, nstore * slot_span).reshape(nstore, slot_span)
    received = fetch_tiles(requests, value_tile_store).reshape(nstore * slot_span, -1)
    for step_index in range(step_count):
        tiles_all.append(received[flat_idx[step_index]])
    results = []
    for step_index in range(step_count):
        per_rows = [
            attend_row(
                queries[:, 0],
                new_keys[:, 0],
                incoming_values[:, 0],
                key_left[0],
                right_key_factor[0],
                chosen[step_index, 0],
                tiles_all[step_index][0],
                lengths[0],
                step_index,
            )
        ]
        results.append(jnp.stack(per_rows))
    return jnp.stack(results)


def plan_kernel(
    share, chosen_ref, keeper_ref, inside_ref, place_ref, asked_ref,
    send_ref, recv_ref, send_sem, recv_sem,
):
    me = lax.axis_index("store")
    count = asked_ref.shape[0]
    barrier = pltpu.get_barrier_semaphore()

    def greet(k, _):
        pl.semaphore_signal(
            barrier, inc=1, device_id={"store": lax.rem(me + k, count)},
            device_id_type=pl.DeviceIdType.MESH,
        )
        return 0

    lax.fori_loop(1, count, greet, 0)
    rows, picks = chosen_ref.shape
    heads, blocks = keeper_ref.shape
    holders = count
    total = holders * share
    block_at = lax.broadcasted_iota(jnp.int32, (rows, blocks), 1)
    chosen = chosen_ref[...]
    hit = jnp.zeros((rows, blocks), jnp.int32)
    for pick in range(picks):
        hit = jnp.where(chosen[:, pick : pick + 1] == block_at, 1, hit)
    keeper = jnp.concatenate([keeper_ref[...]] * (rows // heads), 0)
    kept = jnp.where(hit == 1, keeper, -1)
    before = (
        lax.broadcasted_iota(jnp.int32, (blocks, blocks), 0)
        < lax.broadcasted_iota(jnp.int32, (blocks, blocks), 1)
    ).astype(jnp.float32).astype(jnp.bfloat16)
    mine = [jnp.where(kept == holder, 1.0, 0.0) for holder in range(holders)]
    counts = jnp.dot(
        jnp.concatenate(mine, 0).astype(jnp.bfloat16), before, preferred_element_type=jnp.float32
    )
    order = jnp.zeros((rows, blocks), jnp.float32)
    for holder in range(holders):
        order = order + mine[holder] * counts[holder * rows : (holder + 1) * rows]
    place = jnp.where(hit == 1, keeper * share + order.astype(jnp.int32), -1)
    place_ref[...] = place
    inside = inside_ref[...]
    low = (inside & 255).astype(jnp.float32)
    middle = ((inside >> 8) & 255).astype(jnp.float32)
    high = (inside >> 16).astype(jnp.float32)
    slot_at = lax.broadcasted_iota(jnp.int32, (total, blocks), 0)
    moved = []
    for row in range(rows):
        head = row % heads
        digits = jnp.concatenate(
            [low[head : head + 1], middle[head : head + 1], high[head : head + 1],
             jnp.zeros((5, blocks), jnp.float32)], 0
        ).astype(jnp.bfloat16)
        table = jnp.where(place[row : row + 1] == slot_at, 1.0, 0.0).astype(jnp.bfloat16)
        found = lax.dot_general(
            digits, table, (((1,), (1,)), ((), ())), preferred_element_type=jnp.float32
        ).astype(jnp.int32)
        found = found[0:1] + found[1:2] * 256 + found[2:3] * 65536
        moved.append(pltpu.roll(found, row * share, 1) if row else found)
    moved = jnp.concatenate(moved, 0)
    own_lanes = (
        lax.broadcasted_iota(jnp.int32, (rows, total), 1) // share
        == lax.broadcasted_iota(jnp.int32, (rows, total), 0)
    )
    for holder in range(holders):
        turned = pltpu.roll(moved, total - holder * share, 1) if holder else moved
        send_ref[holder] = jnp.sum(jnp.where(own_lanes, turned, 0), 0, keepdims=True)

    def copy(k):
        peer = lax.rem(me + k, holders)
        return pltpu.make_async_remote_copy(
            src_ref=send_ref.at[peer],
            dst_ref=recv_ref.at[k],
            send_sem=send_sem.at[k],
            recv_sem=recv_sem.at[k],
            device_id={"store": peer},
            device_id_type=pl.DeviceIdType.MESH,
        )

    pl.semaphore_wait(barrier, holders - 1)
    for k in range(1, holders):
        copy(k).start()
    asked_ref[0] = send_ref[me]
    for k in range(1, holders):
        copy(k).wait_recv()
        asked_ref[k] = recv_ref[k]
    for k in range(1, holders):
        copy(k).wait_send()


def weigh_kernel(
    share, length_ref, query_ref, fresh_key_ref, fresh_value_ref, left_ref, right_ref, place_ref,
    coarse_cos_ref, coarse_sin_ref, fine_cos_ref, fine_sin_ref,
    wire_ref, fresh_ref, raw_ref, score_ref, sent_ref,
):
    j = pl.program_id(0)
    in_block = pl.num_programs(0)
    heads, both, _ = query_ref.shape
    blocks = left_ref.shape[1]
    steps = place_ref.shape[0] // heads
    group = both // steps
    holders = wire_ref.shape[0]
    half = HEAD_SIZE // 2
    scale = HEAD_SIZE ** (-0.5)

    raw_ref[...] = lax.dot_general(
        right_ref[...], left_ref[0], (((1,), (1,)), ((), ())), preferred_element_type=jnp.float32
    )
    fine_cos, fine_sin = fine_cos_ref[0], fine_sin_ref[0]
    cosine = coarse_cos_ref[...] * fine_cos - coarse_sin_ref[...] * fine_sin
    sine = coarse_sin_ref[...] * fine_cos + coarse_cos_ref[...] * fine_sin
    for head in range(heads):
        first = raw_ref[head * HEAD_SIZE : head * HEAD_SIZE + half]
        second = raw_ref[head * HEAD_SIZE + half : (head + 1) * HEAD_SIZE]
        keys = jnp.concatenate(
            [first * cosine - second * sine, second * cosine + first * sine], 0
        ).astype(jnp.bfloat16)
        score_ref[head, j] = (
            jnp.dot(query_ref[head], keys, preferred_element_type=jnp.float32) * scale
        )

    @pl.when(j == in_block - 1)
    def _():
        length = length_ref[0]
        tokens = score_ref.shape[1]
        block_at = lax.broadcasted_iota(jnp.int32, (both, blocks), 1)
        slot_at = lax.broadcasted_iota(jnp.int32, (holders * share, blocks), 0)
        fresh_keep = (
            lax.broadcasted_iota(jnp.int32, (both, 8), 1)
            <= lax.broadcasted_iota(jnp.int32, (both, 8), 0) // group
        )

        def one_head(head, _):
            query = query_ref[head]
            place = jnp.concatenate(
                [place_ref[pl.ds(s * heads + head, 1)] for s in range(steps)], 0
            )
            place_rows = jnp.concatenate(
                [jnp.broadcast_to(place[s : s + 1], (group, blocks)) for s in range(steps)], 0
            )
            inside_at = jnp.where(place_rows >= 0, block_at * tokens, length)
            scores = [
                jnp.where(inside_at + t < length, score_ref[head, t], -jnp.inf)
                for t in range(tokens)
            ]
            fresh = lax.dot_general(
                query, fresh_key_ref[head], (((1,), (1,)), ((), ())),
                preferred_element_type=jnp.float32,
            ) * scale
            fresh = jnp.where(fresh_keep, fresh, -jnp.inf)
            top = scores[0]
            for t in range(1, tokens):
                top = jnp.maximum(top, scores[t])
            highest = jnp.maximum(
                jnp.max(top, -1, keepdims=True), jnp.max(fresh, -1, keepdims=True)
            )
            powers = [jnp.exp(score - highest) for score in scores]
            fresh_power = jnp.exp(fresh - highest)
            total = powers[0]
            for t in range(1, tokens):
                total = total + powers[t]
            denominator = jnp.sum(total, -1, keepdims=True) + jnp.sum(
                fresh_power, -1, keepdims=True
            )
            weights = [power / denominator for power in powers]
            fresh_weight = (fresh_power / denominator).astype(jnp.bfloat16)
            fresh_part = jnp.dot(
                fresh_weight, fresh_value_ref[head], preferred_element_type=jnp.float32
            )
            for s in range(steps):
                fresh_ref[s, head] = fresh_part[s * group : (s + 1) * group]
            for s in range(steps):
                table = jnp.where(place[s : s + 1] == slot_at, 1.0, 0.0).astype(jnp.bfloat16)
                stacked = jnp.concatenate(
                    [weight[s * group : (s + 1) * group] for weight in weights], 0
                ).astype(jnp.bfloat16)
                routed = lax.dot_general(
                    table, stacked, (((1,), (1,)), ((), ())), preferred_element_type=jnp.float32
                )
                at = pl.multiple_of((s * heads + head) * share, share)
                sent_ref[:, pl.ds(at, share), :] = routed.reshape(holders, share, tokens * group)
            return 0

        lax.fori_loop(0, heads, one_head, 0)
        for holder in range(holders):
            wire_ref[holder] = sent_ref[holder].T.astype(jnp.bfloat16)


def meet_kernel(
    share, wire_ref, fresh_ref, tiles_ref, out_ref,
    got_ref, part_ref, back_ref, block_ref,
    tile_sem, weight_send, weight_recv, part_send, part_recv,
):
    holders, lines, lanes = wire_ref.shape
    rows = out_ref.shape[0]
    in_block = block_ref.shape[2] // HEAD_SIZE
    group = lines // in_block
    me = lax.axis_index("store")

    def tile_copy(k):
        return pltpu.make_async_copy(
            tiles_ref.at[pl.ds(k * lanes, lanes)],
            block_ref.at[k],
            tile_sem.at[k],
        )

    def weight_copy(k):
        peer = lax.rem(me + k, holders)
        return pltpu.make_async_remote_copy(
            src_ref=wire_ref.at[peer],
            dst_ref=got_ref.at[k],
            send_sem=weight_send.at[k],
            recv_sem=weight_recv.at[k],
            device_id={"store": peer},
            device_id_type=pl.DeviceIdType.MESH,
        )

    def part_copy(k):
        peer = lax.rem(me - k + holders, holders)
        return pltpu.make_async_remote_copy(
            src_ref=part_ref.at[k],
            dst_ref=back_ref.at[k],
            send_sem=part_send.at[k],
            recv_sem=part_recv.at[k],
            device_id={"store": peer},
            device_id_type=pl.DeviceIdType.MESH,
        )

    barrier = pltpu.get_barrier_semaphore()

    def greet(k, _):
        pl.semaphore_signal(
            barrier, inc=1, device_id={"store": lax.rem(me + k, holders)},
            device_id_type=pl.DeviceIdType.MESH,
        )
        return 0

    lax.fori_loop(1, holders, greet, 0)
    far_first = sorted(range(1, holders), key=lambda k: abs(2 * k - holders))
    for k in [0] + far_first:
        tile_copy(k).start()
    pl.semaphore_wait(barrier, holders - 1)
    for k in far_first:
        weight_copy(k).start()

    same = (
        lax.broadcasted_iota(jnp.int32, (rows, lanes), 0) // group
        == lax.broadcasted_iota(jnp.int32, (rows, lanes), 1) // share
    )

    def partial(weight, k):
        weight = weight.astype(jnp.float32)
        spread = [
            jnp.where(
                same, jnp.concatenate([weight[j * group : (j + 1) * group]] * (rows // group), 0), 0.0
            ).astype(jnp.bfloat16)
            for j in range(in_block)
        ]
        values = [
            block_ref[k, :, j * HEAD_SIZE : (j + 1) * HEAD_SIZE] for j in range(in_block)
        ]
        return jnp.dot(
            jnp.concatenate(spread, 1),
            jnp.concatenate(values, 0),
            preferred_element_type=jnp.float32,
        )

    tile_copy(0).wait()
    own = partial(wire_ref[me], 0) + fresh_ref[...]

    for at in range(0, holders - 1, 3):
        trio = far_first[at : at + 3]
        for k in trio:
            tile_copy(k).wait()
            weight_copy(k).wait_recv()
        parts = [partial(got_ref[k], k).astype(jnp.bfloat16) for k in trio]
        for k, part in zip(trio, parts):
            part_ref[k] = part
        for k in trio:
            part_copy(k).start()

    def collect(k, total):
        part_copy(k).wait_recv()
        return total + back_ref[k].astype(jnp.float32)

    out_ref[...] = lax.fori_loop(1, holders, collect, own).astype(jnp.bfloat16)

    def finish(k, _):
        weight_copy(k).wait_send()
        part_copy(k).wait_send()
        return 0

    lax.fori_loop(1, holders, finish, 0)


def routed_device(
    queries, new_keys, incoming_values, key_left, right_key_factor, value_tile_store, slot_map,
    chosen, lengths,
):
    holders = lax.axis_size("store")
    steps, _, heads, picks = chosen.shape
    blocks = slot_map.shape[2]
    share = max(1, blocks // holders // 4)
    pool_here = value_tile_store.shape[0]
    group = queries.shape[2] // HEAD_SIZE // heads
    rank = key_left.shape[2]
    slots = steps * heads * share
    keeper = slot_map[0] // pool_here
    inside = slot_map[0] % pool_here
    place, asked = pl.pallas_call(
        functools.partial(plan_kernel, share),
        out_shape=(
            jax.ShapeDtypeStruct((steps * heads, blocks), jnp.int32),
            jax.ShapeDtypeStruct((holders, 1, slots), jnp.int32),
        ),
        scratch_shapes=[
            pltpu.VMEM((holders, 1, slots), jnp.int32),
            pltpu.VMEM((holders, 1, slots), jnp.int32),
            pltpu.SemaphoreType.DMA((holders,)),
            pltpu.SemaphoreType.DMA((holders,)),
        ],
        compiler_params=pltpu.CompilerParams(collective_id=1, has_side_effects=True),
        name="plan",
    )(chosen[:, 0].reshape(steps * heads, picks), keeper, inside)

    length = lengths[0]
    query = apply_rotary(
        queries[:, 0].reshape(steps, heads * group, HEAD_SIZE).astype(jnp.float32),
        (length + jnp.arange(steps, dtype=jnp.int32))[:, None],
    ).astype(jnp.bfloat16)
    query = query.reshape(steps, heads, group, HEAD_SIZE).transpose(1, 0, 2, 3)
    query = query.reshape(heads, steps * group, HEAD_SIZE)
    fresh_key = apply_rotary(
        new_keys[:, 0].reshape(steps, heads, HEAD_SIZE).astype(jnp.float32),
        (length + jnp.arange(steps, dtype=jnp.int32))[:, None],
    ).astype(jnp.bfloat16)
    extra = ((0, 0), (0, 8 - steps), (0, 0))
    fresh_key = jnp.pad(fresh_key.transpose(1, 0, 2), extra)
    fresh_value = jnp.pad(
        incoming_values[:, 0].reshape(steps, heads, HEAD_SIZE).transpose(1, 0, 2), extra
    )
    left = key_left[0].reshape(blocks, BLOCK_TOKENS, rank).transpose(1, 0, 2)

    half = HEAD_SIZE // 2
    inverse = ROPE_BASE ** (-(np.arange(half, dtype=np.float32) * 2.0 / HEAD_SIZE))
    coarse = inverse[:, None] * (np.arange(blocks) * BLOCK_TOKENS)[None, :]
    fine = (np.arange(BLOCK_TOKENS)[:, None] * inverse[None, :])[..., None]
    constant = lambda table: jnp.asarray(table.astype(np.float32))
    whole = lambda *shape: pl.BlockSpec(shape, lambda j: (0,) * len(shape))
    per_token = lambda *shape: pl.BlockSpec((1,) + shape, lambda j: (j, 0, 0))
    wire, fresh = pl.pallas_call(
        functools.partial(weigh_kernel, share),
        grid=(BLOCK_TOKENS,),
        in_specs=[
            pl.BlockSpec(memory_space=pltpu.SMEM),
            whole(heads, steps * group, HEAD_SIZE),
            whole(heads, 8, HEAD_SIZE),
            whole(heads, 8, HEAD_SIZE),
            per_token(blocks, rank),
            whole(heads * HEAD_SIZE, rank),
            whole(steps * heads, blocks),
            whole(half, blocks),
            whole(half, blocks),
            per_token(half, 1),
            per_token(half, 1),
        ],
        out_specs=(
            whole(holders, BLOCK_TOKENS * group, slots),
            whole(steps, heads, group, HEAD_SIZE),
        ),
        out_shape=(
            jax.ShapeDtypeStruct((holders, BLOCK_TOKENS * group, slots), jnp.bfloat16),
            jax.ShapeDtypeStruct((steps, heads, group, HEAD_SIZE), jnp.float32),
        ),
        scratch_shapes=[
            pltpu.VMEM((heads * HEAD_SIZE, blocks), jnp.float32),
            pltpu.VMEM((heads, BLOCK_TOKENS, steps * group, blocks), jnp.float32),
            pltpu.VMEM((holders, slots, BLOCK_TOKENS * group), jnp.float32),
        ],
        cost_estimate=pl.CostEstimate(
            flops=4 * heads * blocks * BLOCK_TOKENS * rank * HEAD_SIZE,
            bytes_accessed=8 << 20,
            transcendentals=0,
        ),
        name="weigh",
    )(
        lengths, query, fresh_key, fresh_value, left, right_key_factor[0].T,
        place,
        constant(np.cos(coarse)), constant(np.sin(coarse)),
        constant(np.cos(fine)), constant(np.sin(fine)),
    )
    tiles = value_tile_store.at[asked.reshape(-1)].get(mode="promise_in_bounds")
    rows = steps * heads * group
    lines = BLOCK_TOKENS * group
    in_vmem = pl.BlockSpec(memory_space=pltpu.VMEM)
    attended = pl.pallas_call(
        functools.partial(meet_kernel, share),
        in_specs=[in_vmem, in_vmem, pl.BlockSpec(memory_space=pl.ANY)],
        out_specs=in_vmem,
        out_shape=jax.ShapeDtypeStruct((rows, HEAD_SIZE), jnp.bfloat16),
        scratch_shapes=[
            pltpu.VMEM((holders, lines, slots), jnp.bfloat16),
            pltpu.VMEM((holders, rows, HEAD_SIZE), jnp.bfloat16),
            pltpu.VMEM((holders, rows, HEAD_SIZE), jnp.bfloat16),
            pltpu.VMEM((holders, slots, BLOCK_TOKENS * HEAD_SIZE), jnp.bfloat16),
        ]
        + [pltpu.SemaphoreType.DMA((holders,))] * 5,
        compiler_params=pltpu.CompilerParams(collective_id=0, has_side_effects=True),
        name="meet",
    )(wire, fresh.reshape(rows, HEAD_SIZE), tiles)
    return attended.reshape(steps, 1, -1)


def solution(mesh):
    in_specs = (
        P(None, ("groups", "store"), None),
        P(None, ("groups", "store"), None),
        P(None, ("groups", "store"), None),
        P(("groups", "store"), None, None),
        P(("groups", "store"), None, None),
        P(("groups", "store"), None),
        P(("groups", "store"), None, None),
        P(None, ("groups", "store"), None, None),
        P(("groups", "store")),
    )
    out_specs = P(None, ("groups", "store"), None)
    def body(*args):
        share = max(1, args[6].shape[2] // mesh.shape["store"] // 4)
        square = args[7].shape[0] * args[7].shape[2] == mesh.shape["store"]
        return (routed_device if share == 8 and square else per_device)(*args)

    return jax.shard_map(
        body, mesh=mesh, in_specs=in_specs, out_specs=out_specs, check_vma=False
    )
```

profile of v0, /device:TPU:0, one launch (start us, length us, event | category | flops | bytes accessed | tf_op | source)
XLA Modules:
  0.0 75.9 jit_solution(18309504182285561434)
XLA Ops:
  0.0 0.0 copy-start
  0.7 0.1 multiply_cosine_fusion
  0.8 0.8 %convert_bitcast_fusion = f32[1,2,64,128]{3,1,2,0:T(2,128)S(1)} fusion(bf16[2,1,8192]{2,0,1:T(2,128)(2,1)} %param.13), kind=kLoop, calls=%fused_computation.3 | loop fusion | flops 16384 | bytes 98304
  1.6 0.1 fusion
  1.7 0.7 copy_bitcast_fusion.2.query_ref
  2.4 0.7 bitcast_convert_fusion
  3.1 0.1 subtract_convert_fusion.1
  3.2 0.1 maximum_bitcast_fusion.1
  3.3 0.6 pad.7.fresh_key_ref
  3.9 1.3 %add_select_fusion = (s32[8,512]{1,0:T(8,128)}, s32[8,512]{1,0:T(8,128)}) fusion(s32[1,8,512]{2,1,0:T(8,128)} %param.19), kind=kLoop, calls=%fused_computation.11 | loop fusion | flops 77824 | bytes 49152 | tf_op jit(solution)/shard_map/jit(remainder)/select_n | solution.py:492
  5.2 10.7 %plan.1 = (s32[16,512]{1,0:T(8,128)}, s32[16,1,128]{2,1,0:T(1,128)}) custom-call(s32[16,64]{1,0:T(8,128)} %bitcast.70, s32[8,512]{1,0:T(8,128)} %get-tuple-element.16.keeper_ref, s32[8,512]{1,0:T(8,128)} %get-tuple-element.15.inside_ref), custom_call_target="tpu_custom_call" | custom-call | tf_op jit(solution)/shard_map/plan/pallas_call | solution.py:493
  15.9 0.0 copy-start.2
  16.0 3.1 %copy.16 = bf16[1,4096,160]{2,1,0:T(8,128)(2,1)S(1)} copy(bf16[1,4096,160]{1,2,0:T(8,128)(2,1)} %param.16) | data formatting | bytes 2621440 | tf_op args[3]
  19.1 1.8 %copy.23 = bf16[512,8,160]{2,0,1:T(8,128)(2,1)} copy(bf16[512,8,160]{2,1,0:T(8,128)(2,1)S(1)} %bitcast.64) | data formatting | bytes 2621440 | tf_op jit(solution)/shard_map/reshape;squeeze | solution.py:525
  20.8 0.0 copy-done
  20.8 1.0 %copy.18 = bf16[1,160,1024]{1,2,0:T(8,128)(2,1)} copy(bf16[1,160,1024]{2,1,0:T(8,128)(2,1)S(1)} %copy-done) | data formatting | bytes 655360 | tf_op args[4]
  21.8 0.0 copy-done.2
  21.8 0.6 pad.8.fresh_value_ref
  22.4 0.0 copy-start.1
  22.5 12.9 %weigh.1 = (bf16[16,64,128]{2,1,0:T(8,128)(2,1)}, f32[2,8,8,128]{3,2,1,0:T(8,128)}) custom-call(s32[1]{0:T(128)} %copy.25.length_ref, bf16[8,16,128]{2,1,0:T(8,128)(2,1)} %copy_bitcast_fusion.2.query_ref, bf16[8,8,128]{2,1,0:T(8,128)(2,1)} %pad.7.fresh_key_ref, bf16[8,8,128]{2,1,0:T(8,128)(2,1)} %pad.8.fresh_value_ref, bf16[8,512,160]{2,1,0:T(8,128)(2,1)} %bitcast.65, ...), custom_call_target="tpu_custom_call" | custom-call | flops 2684354560 | bytes 8388608 | tf_op jit(solution)/shard_map/weigh/pallas_call | solution.py:534
  35.4 0.0 copy-done.1
  35.4 15.4 %gather_fusion = bf16[2048,1024]{1,0:T(8,128)(2,1)} fusion(bf16[4096,1024]{1,0:T(8,128)(2,1)} %param.18, s32[2048]{0:T(1024)S(1)} %broadcast_clamp_fusion), kind=kCustom, calls=%fused_computation | custom fusion | bytes 8396800 | tf_op jit(solution)/shard_map/gather | solution.py:575
  50.8 23.6 %meet.1 = bf16[128,128]{1,0:T(8,128)(2,1)} custom-call(bf16[16,64,128]{2,1,0:T(8,128)(2,1)} %get-tuple-element.10.wire_ref, f32[128,128]{1,0:T(8,128)} %bitcast.68, bf16[2048,1024]{1,0:T(8,128)(2,1)} %gather_fusion), custom_call_target="tpu_custom_call" | custom-call | tf_op jit(solution)/shard_map/meet/pallas_call | solution.py:579
  74.5 1.4 %reshape.123 = bf16[2,1,8192]{2,0,1:T(2,128)(2,1)} reshape(bf16[128,128]{1,0:T(8,128)(2,1)} %meet.1) | data formatting | bytes 65536 | tf_op jit(solution)/shard_map/reshape | solution.py:594
  (5 shorter events, 0.0 us)
Async XLA Ops:
  0.0 20.8 %copy-start = (bf16[1,160,1024]{2,1,0:T(8,128)(2,1)S(1)}, bf16[1,160,1024]{2,1,0:T(8,128)(2,1)}, u32[]{:S(2)}) copy-start(bf16[1,160,1024]{2,1,0:T(8,128)(2,1)} %param.17) | copy-start | bytes 983044
  15.9 5.9 %copy-start.2 = (bf16[2,1,1024]{2,0,1:T(2,128)(2,1)S(1)}, bf16[2,1,1024]{2,0,1:T(2,128)(2,1)}, u32[]{:S(2)}) copy-start(bf16[2,1,1024]{2,0,1:T(2,128)(2,1)} %param.15) | copy-start | bytes 12292
  22.4 12.9 %copy-start.1 = (s32[16,1,128]{2,1,0:T(1,128)S(1)}, s32[16,1,128]{2,1,0:T(1,128)}, u32[]{:S(2)}) copy-start(s32[16,1,128]{2,1,0:T(1,128)} %get-tuple-element.12) | copy-start | bytes 24580
where the time goes:
time: 76.5 us; the launch traced here: 75.9 us
  Pallas kernels  47.3 us (62%)
  local copies, waits for them, and re-layouts  23.9 us (31%)
  other arithmetic  3.9 us (5%)
  between operations  0.79 us (1%)
    pallas_call x1, Pallas kernels, routed_device(): pl.pallas_call(functools.partial(meet_kernel, share), in_specs=[in_vmem,...  23.6 us
    gather x1, local copies, waits for them, and re-layouts, routed_device(): tiles = value_tile_store.at[asked.reshape(-1)].get(mode='promise_in_bounds')  15.4 us
    pallas_call x1, Pallas kernels, routed_device(): pl.pallas_call(functools.partial(weigh_kernel, share), grid=(BLOCK_TOKENS...  12.9 us
    pallas_call x1, Pallas kernels, routed_device(): pl.pallas_call(functools.partial(plan_kernel, share), out_shape=(jax.Shap...  10.7 us
    unnamed x9, local copies, waits for them, and re-layouts  4.13 us
    another operation x1, local copies, waits for them, and re-layouts, routed_device(): left = key_left[0].reshape(blocks, BLOCK_TOKENS, rank).transpose(1, 0, 2)  1.76 us

commit v1 on v0

v1 whole, which is shorter than its diff:
```python
import functools

import jax
import jax.numpy as jnp
import numpy as np
from jax import lax
from jax.experimental import pallas as pl
from jax.experimental.pallas import tpu as pltpu
from jax.sharding import PartitionSpec as P

KEY_VALUE_HEADS = 8
HEAD_SIZE = 128
BLOCK_TOKENS = 8


ROPE_BASE = 500000.0


def apply_rotary(tensor, token_positions):
    half_dim = tensor.shape[-1] // 2
    inverse = ROPE_BASE ** (-(jnp.arange(half_dim, dtype=jnp.float32) * 2.0 / tensor.shape[-1]))
    angles = jnp.asarray(token_positions).astype(jnp.float32)[..., None] * inverse
    cosine = jnp.cos(angles)
    sine_vals = jnp.sin(angles)
    first_half = tensor[..., :half_dim]
    second_half = tensor[..., half_dim:]
    return jnp.concatenate(
        [
            first_half * cosine - second_half * sine_vals,
            second_half * cosine + first_half * sine_vals,
        ],
        -1,
    )


def fetch_tiles(requests, value_tile_store):
    tile_row_index = jnp.take(
        value_tile_store,
        lax.all_to_all(requests, "store", split_axis=0, concat_axis=0, tiled=True),
        axis=0,
    )
    return lax.all_to_all(tile_row_index, "store", split_axis=0, concat_axis=0, tiled=True)


def build_requests(flat_idx, inside, total):
    buffer = jnp.zeros((total,), jnp.int32)
    return buffer.at[flat_idx.reshape(-1)].set(inside.reshape(-1))


def attend_row(
    query_full,
    incoming_keys_full,
    incoming_values_full,
    left_rows,
    right_factor_rows,
    block_numbers,
    tile_row_index,
    length,
    step_index,
):
    query_group_size = query_full.shape[-1] // HEAD_SIZE // KEY_VALUE_HEADS
    every_head = query_group_size * KEY_VALUE_HEADS
    selected_count = block_numbers.shape[1]
    score_scale = HEAD_SIZE ** (-0.5)
    right_factor_heads = right_factor_rows.reshape(
        right_factor_rows.shape[0], KEY_VALUE_HEADS, HEAD_SIZE
    )
    token_positions = (
        block_numbers[:, :, None] * BLOCK_TOKENS + jnp.arange(BLOCK_TOKENS, dtype=jnp.int32)
    ).reshape(KEY_VALUE_HEADS, selected_count * BLOCK_TOKENS)
    picked = left_rows[token_positions]
    raw_keys = jnp.einsum(
        "htr,rhd->htd", picked, right_factor_heads, preferred_element_type=jnp.float32
    )
    cache_keys = apply_rotary(raw_keys, token_positions).astype(jnp.bfloat16)
    rotated_query = apply_rotary(
        query_full[step_index].reshape(every_head, HEAD_SIZE).astype(jnp.float32),
        length + step_index,
    ).astype(jnp.bfloat16)
    current_position = (length + jnp.arange(step_index + 1, dtype=jnp.int32))[:, None]
    current_keys = apply_rotary(
        incoming_keys_full[: step_index + 1]
        .reshape(step_index + 1, KEY_VALUE_HEADS, HEAD_SIZE)
        .astype(jnp.float32),
        current_position,
    ).astype(jnp.bfloat16)
    current_keys = jnp.transpose(current_keys, (1, 0, 2))
    current_values = jnp.transpose(
        incoming_values_full[: step_index + 1].reshape(step_index + 1, KEY_VALUE_HEADS, HEAD_SIZE),
        (1, 0, 2),
    )
    local_values = tile_row_index.reshape(KEY_VALUE_HEADS, selected_count * BLOCK_TOKENS, HEAD_SIZE)
    grouped_queries = rotated_query.reshape(KEY_VALUE_HEADS, query_group_size, HEAD_SIZE)
    cache_scores = (
        jnp.einsum("hgd,htd->hgt", grouped_queries, cache_keys, preferred_element_type=jnp.float32)
        * score_scale
    )
    inside_len = token_positions < length
    cache_scores = jnp.where(inside_len[:, None, :], cache_scores, -jnp.inf)
    fresh_scores = (
        jnp.einsum(
            "hgd,hnd->hgn", grouped_queries, current_keys, preferred_element_type=jnp.float32
        )
        * score_scale
    )
    highest = jnp.maximum(
        jnp.max(cache_scores, -1, keepdims=True), jnp.max(fresh_scores, -1, keepdims=True)
    )
    cache_exp = jnp.exp(cache_scores - highest)
    fresh_exp = jnp.exp(fresh_scores - highest)
    denominator = jnp.sum(cache_exp, -1, keepdims=True) + jnp.sum(fresh_exp, -1, keepdims=True)
    cache_weight = (cache_exp / denominator).astype(jnp.bfloat16)
    fresh_weight = (fresh_exp / denominator).astype(jnp.bfloat16)
    attended = jnp.einsum(
        "hgt,htd->hgd", cache_weight, local_values, preferred_element_type=jnp.float32
    )
    attended = attended + jnp.einsum(
        "hgn,hnd->hgd", fresh_weight, current_values, preferred_element_type=jnp.float32
    )
    return attended.reshape(every_head * HEAD_SIZE).astype(jnp.bfloat16)


def per_device(
    queries,
    new_keys,
    incoming_values,
    key_left,
    right_key_factor,
    value_tile_store,
    slot_map,
    chosen,
    lengths,
):
    nstore = lax.axis_size("store")
    local_rows = key_left.shape[0]
    nchunk = slot_map.shape[2]
    step_count = chosen.shape[0]
    selected_count = chosen.shape[3]
    keeper_share = max(1, nchunk // nstore // 4)
    tile_limit = local_rows * KEY_VALUE_HEADS * keeper_share
    pool_here = value_tile_store.shape[0]
    slot_numbers = jnp.take_along_axis(
        jnp.broadcast_to(slot_map[None], (step_count,) + slot_map.shape), chosen, axis=3
    )
    tile_keeper = slot_numbers // pool_here
    inside = slot_numbers % pool_here
    matched = tile_keeper[..., :, None] == tile_keeper[..., None, :]
    earlier = jnp.arange(selected_count)[None, :] < jnp.arange(selected_count)[:, None]
    order_in = jnp.sum(jnp.logical_and(matched, earlier), -1)
    row_head = (
        jnp.arange(local_rows, dtype=jnp.int32)[:, None, None] * KEY_VALUE_HEADS
        + jnp.arange(KEY_VALUE_HEADS, dtype=jnp.int32)[None, :, None]
    )
    position = row_head * keeper_share + order_in
    tiles_all = []
    slot_span = step_count * tile_limit
    flat_idx = (
        tile_keeper * slot_span
        + jnp.arange(step_count, dtype=jnp.int32)[:, None, None, None] * tile_limit
        + position
    )
    requests = build_requests(flat_idx, inside, nstore * slot_span).reshape(nstore, slot_span)
    received = fetch_tiles(requests, value_tile_store).reshape(nstore * slot_span, -1)
    for step_index in range(step_count):
        tiles_all.append(received[flat_idx[step_index]])
    results = []
    for step_index in range(step_count):
        per_rows = [
            attend_row(
                queries[:, 0],
                new_keys[:, 0],
                incoming_values[:, 0],
                key_left[0],
                right_key_factor[0],
                chosen[step_index, 0],
                tiles_all[step_index][0],
                lengths[0],
                step_index,
            )
        ]
        results.append(jnp.stack(per_rows))
    return jnp.stack(results)


def fused_kernel(
    share, pool_here,
    length_ref, turn_cos_ref, turn_sin_ref, query_ref, new_key_ref, new_value_ref,
    chosen_ref, slot_ref, right_ref, coarse_cos_ref, coarse_sin_ref, fine_cos_ref, fine_sin_ref,
    spread_ref, left_hbm, regroup_hbm, pool_hbm,
    out_ref,
    left_ref, regroup_ref, pool_ref, send_ref, ask_ref, asked_ref, row_ref,
    place_ref, sign_ref, rotated_ref, fresh_key_ref, fresh_value_ref, flip_ref, token_ref,
    cosine_ref, sine_ref, score_ref, fresh_ref, routed_ref, wire_ref, got_ref,
    core_out, core_in, side_out, side_in, line_out, line_in, keep_ref,
    left_sem, regroup_sem, pool_sem, row_sem, ask_send, ask_recv, wire_send, wire_recv,
    core_send, core_recv, side_send, side_recv, line_send, line_recv,
):
    me = lax.axis_index("store")
    holders = send_ref.shape[0]
    depth = holders // 4
    rows, picks = chosen_ref.shape
    heads, blocks = slot_ref.shape
    steps = rows // heads
    rank = right_ref.shape[0]
    group = query_ref.shape[1] // HEAD_SIZE // heads
    both = steps * group
    half = HEAD_SIZE // 2
    quad = heads // 2
    scale = HEAD_SIZE ** (-0.5)
    core, side, layer = lax.rem(me, 2), lax.rem(me // 2, 2), me // 4

    def peer(j):
        far, across, ahead = j // (2 * depth), j // depth % 2, j % depth
        return (
            lax.rem(layer + ahead, depth) * 4
            + (1 - side if across else side) * 2
            + (1 - core if far else core)
        )

    def remote(src, dst, send, recv, target):
        return pltpu.make_async_remote_copy(
            src_ref=src, dst_ref=dst, send_sem=send, recv_sem=recv,
            device_id={"store": target}, device_id_type=pl.DeviceIdType.MESH,
        )

    barrier = pltpu.get_barrier_semaphore()

    def greet(k, _):
        pl.semaphore_signal(
            barrier, inc=1, device_id={"store": lax.rem(me + k, holders)},
            device_id_type=pl.DeviceIdType.MESH,
        )
        return 0

    lax.fori_loop(1, holders, greet, 0)

    left_copy = pltpu.make_async_copy(left_hbm, left_ref, left_sem.at[0])
    regroup_copy = pltpu.make_async_copy(regroup_hbm, regroup_ref, regroup_sem.at[0])
    left_copy.start()
    regroup_copy.start()
    octets = pool_here // 8
    pool_copies = [
        pltpu.make_async_copy(
            pool_hbm.at[:, pl.ds(2 * q, 2), pl.ds(HEAD_SIZE * t, HEAD_SIZE)],
            pool_ref.at[pl.ds(q * octets, octets), pl.ds(2 * t, 2), :],
            pool_sem.at[q * BLOCK_TOKENS + t],
        )
        for q in range(4)
        for t in range(BLOCK_TOKENS)
    ]
    for copy in pool_copies:
        copy.start()

    total = holders * share
    block_at = lax.broadcasted_iota(jnp.int32, (rows, blocks), 1)
    chosen = chosen_ref[...]
    hit = jnp.zeros((rows, blocks), jnp.int32)
    for pick in range(picks):
        hit = jnp.where(chosen[:, pick : pick + 1] == block_at, 1, hit)
    slot = slot_ref[...]
    if pool_here & (pool_here - 1) == 0:
        keeper_head = slot >> (pool_here.bit_length() - 1)
        inside = slot & (pool_here - 1)
    else:
        keeper_head = lax.div(slot, jnp.full_like(slot, pool_here))
        inside = slot - keeper_head * pool_here
    sign_ref[...] = (1 - 2 * (inside & 1)).astype(jnp.float32)
    inside = ((inside >> 1) & 3) * octets + (inside >> 3)
    keeper = jnp.concatenate([keeper_head] * steps, 0)
    kept = jnp.where(hit == 1, keeper, -1)
    before = (
        lax.broadcasted_iota(jnp.int32, (blocks, blocks), 0)
        < lax.broadcasted_iota(jnp.int32, (blocks, blocks), 1)
    ).astype(jnp.float32).astype(jnp.bfloat16)
    mine = [jnp.where(kept == holder, 1.0, 0.0) for holder in range(holders)]
    counts = jnp.dot(
        jnp.concatenate(mine, 0).astype(jnp.bfloat16), before, preferred_element_type=jnp.float32
    )
    order = jnp.zeros((rows, blocks), jnp.float32)
    for holder in range(holders):
        order = order + mine[holder] * counts[holder * rows : (holder + 1) * rows]
    place = jnp.where(hit == 1, keeper * share + order.astype(jnp.int32), -1)
    place_ref[...] = place
    low = (inside & 255).astype(jnp.float32)
    middle = ((inside >> 8) & 255).astype(jnp.float32)
    high = (inside >> 16).astype(jnp.float32)
    slot_at = lax.broadcasted_iota(jnp.int32, (total, blocks), 0)
    moved = []
    for row in range(rows):
        head = row % heads
        digits = jnp.concatenate(
            [low[head : head + 1], middle[head : head + 1], high[head : head + 1],
             jnp.zeros((5, blocks), jnp.float32)], 0
        ).astype(jnp.bfloat16)
        table = jnp.where(place[row : row + 1] == slot_at, 1.0, 0.0).astype(jnp.bfloat16)
        found = lax.dot_general(
            digits, table, (((1,), (1,)), ((), ())), preferred_element_type=jnp.float32
        ).astype(jnp.int32)
        found = found[0:1] + found[1:2] * 256 + found[2:3] * 65536
        moved.append(pltpu.roll(found, row * share, 1) if row else found)
    moved = jnp.concatenate(moved, 0)
    own_lanes = (
        lax.broadcasted_iota(jnp.int32, (rows, total), 1) // share
        == lax.broadcasted_iota(jnp.int32, (rows, total), 0)
    )
    for holder in range(holders):
        turned = pltpu.roll(moved, total - holder * share, 1) if holder else moved
        send_ref[holder] = jnp.sum(jnp.where(own_lanes, turned, 0), 0, keepdims=True)

    def ask_copy(j):
        target = peer(j)
        return remote(
            send_ref.at[target], ask_ref.at[j], ask_send.at[j], ask_recv.at[j], target
        )

    far_first = sorted(
        range(1, holders), key=lambda j: (-(min(j % depth, depth - j % depth)), -j)
    )
    pl.semaphore_wait(barrier, holders - 1)
    for j in far_first:
        ask_copy(j).start()
    ask_ref[0] = send_ref[me]

    spin_cos = [
        jnp.broadcast_to(
            jnp.concatenate([turn_cos_ref[s : s + 1]] * 2, 1), (group, HEAD_SIZE)
        )
        for s in range(steps)
    ]
    spin_sin = [
        jnp.broadcast_to(
            jnp.concatenate([-turn_sin_ref[s : s + 1], turn_sin_ref[s : s + 1]], 1),
            (group, HEAD_SIZE),
        )
        for s in range(steps)
    ]
    query_all = query_ref[...].astype(jnp.float32)
    key_all = new_key_ref[...].astype(jnp.float32)
    value_all = new_value_ref[...].astype(jnp.float32)
    fresh_cos = jnp.concatenate([spin_cos[s][:1] for s in range(steps)] + [spin_cos[0][: 8 - steps]], 0)
    fresh_sin = jnp.concatenate([spin_sin[s][:1] for s in range(steps)] + [spin_sin[0][: 8 - steps]], 0)
    both_cos = jnp.concatenate(spin_cos, 0)
    both_sin = jnp.concatenate(spin_sin, 0)
    empty = jnp.zeros((8 - steps, HEAD_SIZE), jnp.float32)
    for head in range(heads):
        lanes = slice(head * HEAD_SIZE, (head + 1) * HEAD_SIZE)
        flat = jnp.concatenate(
            [
                query_all[s : s + 1, (head * group + g) * HEAD_SIZE : (head * group + g + 1) * HEAD_SIZE]
                for s in range(steps)
                for g in range(group)
            ],
            0,
        )
        rotated_ref[head] = (
            flat * both_cos + pltpu.roll(flat, half, 1) * both_sin
        ).astype(jnp.bfloat16)
        flat = jnp.concatenate([key_all[:, lanes], empty], 0)
        fresh_key_ref[head] = (
            flat * fresh_cos + pltpu.roll(flat, half, 1) * fresh_sin
        ).astype(jnp.bfloat16)
        fresh_value_ref[head] = jnp.concatenate([value_all[:, lanes], empty], 0).astype(
            jnp.bfloat16
        )
        flip_ref[lanes, :] = right_ref[:, lanes].astype(jnp.float32).T.astype(jnp.bfloat16)
    for t in range(BLOCK_TOKENS):
        fine_cos, fine_sin = fine_cos_ref[t], fine_sin_ref[t]
        cosine_ref[t] = coarse_cos_ref[...] * fine_cos - coarse_sin_ref[...] * fine_sin
        sine_ref[t] = coarse_sin_ref[...] * fine_cos + coarse_cos_ref[...] * fine_sin
    left_copy.wait()
    regroup_copy.wait()
    wide = regroup_ref.shape[0]
    low_half = lax.broadcasted_iota(jnp.int32, (rank, 128), 1) < 64
    for m in range(blocks // 128):
        grouped = [
            jnp.dot(
                left_ref[:, (2 * m + n) * wide : (2 * m + n + 1) * wide], regroup_ref[...],
                preferred_element_type=jnp.float32,
            )
            for n in range(2)
        ]
        for t in range(0, BLOCK_TOKENS, 2):
            a, b = (value[:, t * 64 : (t + 2) * 64] for value in grouped)
            for odd, value in enumerate(
                (
                    jnp.where(low_half, a, pltpu.roll(b, 64, 1)),
                    jnp.where(low_half, pltpu.roll(a, 64, 1), b),
                )
            ):
                token_ref[t + odd, :, m * 128 : (m + 1) * 128] = value.astype(jnp.bfloat16)

    length = length_ref[0]
    place_at = lax.broadcasted_iota(jnp.int32, (total, blocks), 0)
    first_token = lax.broadcasted_iota(jnp.int32, (both, blocks), 1) * BLOCK_TOKENS
    fresh_keep = (
        lax.broadcasted_iota(jnp.int32, (both, 8), 1)
        <= lax.broadcasted_iota(jnp.int32, (both, 8), 0) // group
    )
    chunk = min(256, blocks)

    def one_head(head, _):
        query = rotated_ref[head]
        factor = flip_ref[pl.ds(pl.multiple_of(head * HEAD_SIZE, HEAD_SIZE), HEAD_SIZE)]
        for t in range(BLOCK_TOKENS):
            for at in range(0, blocks, chunk):
                lanes = slice(at, at + chunk)
                raw = jnp.dot(
                    factor, token_ref[t, :, lanes], preferred_element_type=jnp.float32
                )
                first, second = raw[:half], raw[half:]
                cosine, sine = cosine_ref[t, :, lanes], sine_ref[t, :, lanes]
                keys = jnp.concatenate(
                    [first * cosine - second * sine, second * cosine + first * sine], 0
                ).astype(jnp.bfloat16)
                score_ref[t, :, lanes] = (
                    jnp.dot(query, keys, preferred_element_type=jnp.float32) * scale
                )
        place = [place_ref[pl.ds(s * heads + head, 1)] for s in range(steps)]
        place_rows = jnp.concatenate(
            [jnp.broadcast_to(place[s], (group, blocks)) for s in range(steps)], 0
        )
        inside_at = jnp.where(place_rows >= 0, first_token, length)
        scores = [
            jnp.where(inside_at + t < length, score_ref[t], -jnp.inf)
            for t in range(BLOCK_TOKENS)
        ]
        fresh = lax.dot_general(
            query, fresh_key_ref[head], (((1,), (1,)), ((), ())),
            preferred_element_type=jnp.float32,
        ) * scale
        fresh = jnp.where(fresh_keep, fresh, -jnp.inf)
        top = scores[0]
        for t in range(1, BLOCK_TOKENS):
            top = jnp.maximum(top, scores[t])
        highest = jnp.maximum(
            jnp.max(top, -1, keepdims=True), jnp.max(fresh, -1, keepdims=True)
        )
        powers = [jnp.exp(score - highest) for score in scores]
        fresh_power = jnp.exp(fresh - highest)
        whole = powers[0]
        for t in range(1, BLOCK_TOKENS):
            whole = whole + powers[t]
        denominator = jnp.sum(whole, -1, keepdims=True) + jnp.sum(
            fresh_power, -1, keepdims=True
        )
        inverse = 1.0 / denominator
        fresh_ref[pl.ds(pl.multiple_of(head * both, both), both)] = jnp.dot(
            (fresh_power * inverse).astype(jnp.bfloat16), fresh_value_ref[head],
            preferred_element_type=jnp.float32,
        )
        sign = sign_ref[pl.ds(head, 1)]
        for s in range(steps):
            table = jnp.where(
                place[s] == place_at, jnp.broadcast_to(sign, (total, blocks)), 0.0
            ).astype(jnp.bfloat16)
            stacked = jnp.concatenate(
                [(power * inverse)[s * group : (s + 1) * group] for power in powers], 0
            ).astype(jnp.bfloat16)
            routed = lax.dot_general(
                stacked, table, (((1,), (1,)), ((), ())), preferred_element_type=jnp.float32
            )
            for t in range(BLOCK_TOKENS):
                routed_ref[t, head, s * group : (s + 1) * group] = routed[
                    t * group : (t + 1) * group
                ]
        return 0

    lane = lax.broadcasted_iota(jnp.int32, (both, total), 1) // share
    middle_t = BLOCK_TOKENS // 2

    def wire_copy(part, j):
        target = peer(j)
        return remote(
            wire_ref.at[part, target], got_ref.at[part, j],
            wire_send.at[part * holders + j], wire_recv.at[part * holders + j], target,
        )

    for part in range(2):
        lax.fori_loop(part * quad, (part + 1) * quad, one_head, 0)
        for upper in range(2):
            cells = [
                routed_ref[upper * middle_t + t, part * quad + h]
                for t in range(middle_t)
                for h in range(quad)
            ]
            step = 1
            while step < holders:
                low_side = lane // step % 2 == 0
                turned = list(cells)
                for at in range(holders):
                    if at // step % 2 == 0:
                        a, b = cells[at], cells[at + step]
                        turned[at] = jnp.where(
                            low_side, a, pltpu.roll(b, step * share, 1)
                        )
                        turned[at + step] = jnp.where(
                            low_side, pltpu.roll(a, total - step * share, 1), b
                        )
                cells = turned
                step *= 2
            for holder in range(holders):
                wire_ref[part, holder, :, upper * total : (upper + 1) * total] = cells[
                    holder
                ].astype(jnp.bfloat16)
        for j in far_first:
            wire_copy(part, j).start()

    for j in range(1, holders):
        ask_copy(j).wait_recv()
    asked_ref[...] = jnp.clip(ask_ref[...], 0, pool_ref.shape[0] - 1)
    row_copy = pltpu.make_async_copy(asked_ref, row_ref, row_sem.at[0])
    row_copy.start()
    row_copy.wait()
    for copy in pool_copies:
        copy.wait()

    early = lax.broadcasted_iota(jnp.int32, (both, HEAD_SIZE), 0) < group

    def partial(part, j):
        if j:
            arrived = got_ref[part, j]
        else:
            arrived = wire_ref[part, me]
        weight = jnp.maximum(
            jnp.dot(arrived, spread_ref[...], preferred_element_type=jnp.float32), 0.0
        )
        results = []
        for h in range(0, quad, 2):
            lhs, columns = [], []
            for h_at in (h, h + 1):
                own = weight[:, h_at * HEAD_SIZE : (h_at + 1) * HEAD_SIZE]
                lhs.append(
                    jnp.concatenate(
                        [jnp.where(early, own, 0.0), jnp.where(early, 0.0, own)], 1
                    ).astype(jnp.bfloat16)
                )
                columns.append(
                    jnp.concatenate(
                        [
                            pool_ref[
                                row_ref[j, 0, (s * heads + part * quad + h_at) * share + n]
                            ]
                            for s in range(steps)
                            for n in range(share)
                        ],
                        0,
                    )
                )
            product = jnp.dot(
                jnp.concatenate(lhs, 0), jnp.concatenate(columns, 1),
                preferred_element_type=jnp.float32,
            )
            results += [product[:both, :HEAD_SIZE], product[both:, HEAD_SIZE:]]
        return jnp.concatenate(results, 0)

    own_core = peer(2 * depth)
    own_side = peer(depth)
    piece = quad * both

    def core_copy(part, across):
        at = part * 2 + across
        return remote(
            core_out.at[at], core_in.at[at], core_send.at[at], core_recv.at[at], own_core
        )

    def side_copy(part):
        return remote(
            side_out.at[part], side_in.at[part], side_send.at[part], side_recv.at[part], own_side
        )

    def line_copy(part, ahead):
        at = part * depth + ahead
        return remote(
            line_out.at[at], line_in.at[at], line_send.at[at], line_recv.at[at],
            lax.rem(layer - ahead + depth, depth) * 4 + side * 2 + core,
        )

    def stage(part, far, across):
        first = far * 2 * depth + across * depth
        js = [first + ahead for ahead in range(depth)]
        for j in js:
            if j:
                wire_copy(part, j).wait_recv()
        return [partial(part, j) for j in js]

    def far_stage(part, across):
        for ahead, value in enumerate(stage(part, 1, across)):
            core_out[part * 2 + across, ahead * piece : (ahead + 1) * piece] = value
        core_copy(part, across).start()

    def side_stage(part):
        values = stage(part, 0, 1)
        core_copy(part, 1).wait_recv()
        for ahead, value in enumerate(values):
            span = slice(ahead * piece, (ahead + 1) * piece)
            side_out[part, span] = (value + core_in[part * 2 + 1, span]).astype(jnp.bfloat16)
        side_copy(part).start()

    def line_stage(part):
        values = stage(part, 0, 0)
        core_copy(part, 0).wait_recv()
        side_copy(part).wait_recv()
        for ahead, value in enumerate(values):
            span = slice(ahead * piece, (ahead + 1) * piece)
            value = value + core_in[part * 2, span] + side_in[part, span].astype(jnp.float32)
            if ahead:
                line_out[part * depth + ahead] = value.astype(jnp.bfloat16)
                line_copy(part, ahead).start()
            else:
                keep_ref[part * piece : (part + 1) * piece] = value

    far_stage(0, 1)
    side_stage(0)
    far_stage(0, 0)
    far_stage(1, 1)
    line_stage(0)
    side_stage(1)
    far_stage(1, 0)
    line_stage(1)

    for part in range(2):
        span = slice(part * piece, (part + 1) * piece)
        value = keep_ref[span] + fresh_ref[span]
        for ahead in range(1, depth):
            line_copy(part, ahead).wait_recv()
            value = value + line_in[part * depth + ahead].astype(jnp.float32)
        keep_ref[span] = value
    for head in range(heads):
        for g in range(group):
            at = (head * group + g) * HEAD_SIZE
            out_ref[:, at : at + HEAD_SIZE] = jnp.concatenate(
                [
                    keep_ref[head * both + s * group + g : head * both + s * group + g + 1]
                    for s in range(steps)
                ],
                0,
            ).astype(jnp.bfloat16)

    for j in range(1, holders):
        ask_copy(j).wait_send()
        for part in range(2):
            wire_copy(part, j).wait_send()
    for part in range(2):
        core_copy(part, 0).wait_send()
        core_copy(part, 1).wait_send()
        side_copy(part).wait_send()
        for ahead in range(1, depth):
            line_copy(part, ahead).wait_send()


def fused_device(
    queries, new_keys, incoming_values, key_left, right_key_factor, value_tile_store, slot_map,
    chosen, lengths,
):
    holders = lax.axis_size("store")
    steps, _, heads, picks = chosen.shape
    blocks = slot_map.shape[2]
    share = max(1, blocks // holders // 4)
    pool_here = value_tile_store.shape[0]
    group = queries.shape[2] // HEAD_SIZE // heads
    rank = key_left.shape[2]
    slots = steps * heads * share
    rows = steps * heads * group
    both = steps * group
    quad = heads // 2
    depth = holders // 4
    piece = quad * both
    half = HEAD_SIZE // 2
    tokens = blocks * BLOCK_TOKENS

    inverse = ROPE_BASE ** (-(jnp.arange(half, dtype=jnp.float32) * 2.0 / HEAD_SIZE))
    angles = (lengths[0] + jnp.arange(steps, dtype=jnp.int32)).astype(jnp.float32)[:, None] * inverse

    inverse = ROPE_BASE ** (-(np.arange(half, dtype=np.float32) * 2.0 / HEAD_SIZE))
    coarse = inverse[:, None] * (np.arange(blocks) * BLOCK_TOKENS)[None, :]
    fine = (np.arange(BLOCK_TOKENS)[:, None] * inverse[None, :])[..., None]
    constant = lambda table: jnp.asarray(table.astype(np.float32))
    wide = BLOCK_TOKENS * 64
    regroup = np.zeros((wide, wide), np.float32)
    for t in range(BLOCK_TOKENS):
        regroup[np.arange(64) * BLOCK_TOKENS + t, t * 64 + np.arange(64)] = 1.0
    spread = np.zeros((BLOCK_TOKENS, quad, share, quad, share, BLOCK_TOKENS, 2), np.float32)
    for t in range(BLOCK_TOKENS):
        for h in range(quad):
            for n in range(share):
                spread[t, h, n, h, n, t] = (1.0, -1.0)
    lines = BLOCK_TOKENS * quad * share
    spread = spread.reshape(lines, 2 * lines)

    vmem = pl.BlockSpec(memory_space=pltpu.VMEM)
    anywhere = pl.BlockSpec(memory_space=pl.ANY)
    bf16, f32 = jnp.bfloat16, jnp.float32
    dma = pltpu.SemaphoreType.DMA
    attended = pl.pallas_call(
        functools.partial(fused_kernel, share, pool_here),
        in_specs=[pl.BlockSpec(memory_space=pltpu.SMEM)] + [vmem] * 13 + [anywhere] * 3,
        out_specs=vmem,
        out_shape=jax.ShapeDtypeStruct((steps, heads * group * HEAD_SIZE), bf16),
        scratch_shapes=[
            pltpu.VMEM((rank, tokens), bf16),
            pltpu.VMEM((wide, wide), bf16),
            pltpu.VMEM((pool_here // 2, 2 * BLOCK_TOKENS, HEAD_SIZE), bf16),
            pltpu.VMEM((holders, 1, slots), jnp.int32),
            pltpu.VMEM((holders, 1, slots), jnp.int32),
            pltpu.VMEM((holders, 1, slots), jnp.int32),
            pltpu.SMEM((holders, 1, slots), jnp.int32),
            pltpu.VMEM((steps * heads, blocks), jnp.int32),
            pltpu.VMEM((heads, blocks), f32),
            pltpu.VMEM((heads, both, HEAD_SIZE), bf16),
            pltpu.VMEM((heads, 8, HEAD_SIZE), bf16),
            pltpu.VMEM((heads, 8, HEAD_SIZE), bf16),
            pltpu.VMEM((heads * HEAD_SIZE, rank), bf16),
            pltpu.VMEM((BLOCK_TOKENS, rank, blocks), bf16),
            pltpu.VMEM((BLOCK_TOKENS, half, blocks), f32),
            pltpu.VMEM((BLOCK_TOKENS, half, blocks), f32),
            pltpu.VMEM((BLOCK_TOKENS, both, blocks), f32),
            pltpu.VMEM((rows, HEAD_SIZE), f32),
            pltpu.VMEM((BLOCK_TOKENS, heads, both, holders * share), f32),
            pltpu.VMEM((2, holders, both, lines), bf16),
            pltpu.VMEM((2, holders, both, lines), bf16),
            pltpu.VMEM((4, depth * piece, HEAD_SIZE), f32),
            pltpu.VMEM((4, depth * piece, HEAD_SIZE), f32),
            pltpu.VMEM((2, depth * piece, HEAD_SIZE), bf16),
            pltpu.VMEM((2, depth * piece, HEAD_SIZE), bf16),
            pltpu.VMEM((2 * depth, piece, HEAD_SIZE), bf16),
            pltpu.VMEM((2 * depth, piece, HEAD_SIZE), bf16),
            pltpu.VMEM((rows, HEAD_SIZE), f32),
            dma((1,)), dma((1,)), dma((4 * BLOCK_TOKENS,)), dma((1,)),
            dma((holders,)), dma((holders,)), dma((2 * holders,)), dma((2 * holders,)),
            dma((4,)), dma((4,)), dma((2,)), dma((2,)), dma((2 * depth,)), dma((2 * depth,)),
        ],
        compiler_params=pltpu.CompilerParams(collective_id=0, has_side_effects=True),
        name="fused",
    )(
        lengths, jnp.cos(angles), jnp.sin(angles), queries[:, 0], new_keys[:, 0],
        incoming_values[:, 0], chosen[:, 0].reshape(steps * heads, picks), slot_map[0],
        right_key_factor[0], constant(np.cos(coarse)), constant(np.sin(coarse)),
        constant(np.cos(fine)), constant(np.sin(fine)), jnp.asarray(spread, bf16),
        key_left[0].T, jnp.asarray(regroup, bf16),
        value_tile_store.reshape(pool_here // 8, 8, -1),
    )
    return attended.reshape(steps, 1, -1)


def solution(mesh):
    in_specs = (
        P(None, ("groups", "store"), None),
        P(None, ("groups", "store"), None),
        P(None, ("groups", "store"), None),
        P(("groups", "store"), None, None),
        P(("groups", "store"), None, None),
        P(("groups", "store"), None),
        P(("groups", "store"), None, None),
        P(None, ("groups", "store"), None, None),
        P(("groups", "store")),
    )
    out_specs = P(None, ("groups", "store"), None)

    def body(*args):
        holders = mesh.shape["store"]
        blocks = args[6].shape[2]
        share = max(1, blocks // holders // 4)
        square = args[7].shape[0] * args[7].shape[2] == holders
        fits = square and share == 8 and holders == 16 and blocks % 128 == 0
        return (fused_device if fits else per_device)(*args)

    return jax.shard_map(
        body, mesh=mesh, in_specs=in_specs, out_specs=out_specs, check_vma=False
    )
```

time: 76.5 us -> 49.3 us (0.64)
  local copies, waits for them, and re-layouts: 23.9 us -> 1.4 us
  other arithmetic: 3.9 us -> 0.71 us
  Pallas kernels: 47.3 us -> 46.3 us
    gather x1 -> x0, local copies, waits for them, and re-layouts: 15.4 us -> none  [routed_device(): tiles = value_tile_store.at[asked.reshape(-1)].get(mode='promise_in_bounds')]
    unnamed x9 -> x1, local copies, waits for them, and re-layouts: 4.13 us -> 1.4 us
    another operation x1 -> x0, local copies, waits for them, and re-layouts: 1.76 us -> none  [routed_device(): left = key_left[0].reshape(blocks, BLOCK_TOKENS, rank).transpose(1, 0, 2)]
    reshape x1 -> x0, local copies, waits for them, and re-layouts: 1.39 us -> none  [routed_device(): return attended.reshape(steps, 1, -1)]
    select_n x2 -> x0, other arithmetic: 1.34 us -> none  [the longest x1 1.33 us: routed_device(): inside = slot_map[0] % pool_here]
    pad x2 -> x0, local copies, waits for them, and re-layouts: 1.21 us -> none  [the longest x1 0.61 us: routed_device(): fresh_key = jnp.pad(fresh_key.transpose(1, 0, 2), extra)]
    pallas_call x3 -> x1, Pallas kernels: 47.3 us -> 46.3 us  [fused_device(): pl.pallas_call(functools.partial(fused_kernel, share, pool_here), in_spec...]
    unnamed x1 -> x0, other arithmetic: 0.79 us -> none
where the time goes in v1:
time: 49.3 us; the launch traced here: 49.1 us
  Pallas kernels  46.3 us (94%)
  local copies, waits for them, and re-layouts  1.4 us (3%)
  other arithmetic  0.71 us (1%)
  between operations  0.67 us (1%)
    pallas_call x1, Pallas kernels, fused_device(): pl.pallas_call(functools.partial(fused_kernel, share, pool_here), in_spec...  46.3 us
    unnamed x1, local copies, waits for them, and re-layouts  1.4 us

profile of v1, /device:TPU:0, one launch (start us, length us, event | category | flops | bytes accessed | tf_op | source)
XLA Modules:
  0.0 49.1 jit_solution(4235073847935742656)
XLA Ops:
  0.7 0.7 %multiply_sine_fusion = (f32[2,64]{1,0:T(2,128)}, f32[2,64]{1,0:T(2,128)}) fusion(f32[64]{0:T(128)S(1)} %negate_power_fusion, f32[2]{0:T(128)S(1)} %add_convert_fusion), kind=kLoop, calls=%fused_computation | loop fusion | flops 128 | bytes 1288 | tf_op jit(solution)/shard_map/sin | solution.py:735
  1.4 46.3 %fused.1 = bf16[2,8192]{1,0:T(2,128)(2,1)} custom-call(s32[1]{0:T(128)} %copy.17.length_ref, f32[2,64]{1,0:T(2,128)} %get-tuple-element.6.turn_cos_ref, f32[2,64]{1,0:T(2,128)} %get-tuple-element.5.turn_sin_ref, bf16[2,8192]{1,0:T(2,128)(2,1)} %bitcast.17, bf16[2,1024]{1,0:T(2,128)(2,1)} %bitcast.20, bf16[2,1024]{1,0:T(2,128)(2,1)} %bitcast.21, ...), custom_call_target="tpu_custom_call" | custom-call | tf_op jit(solution)/shard_map/fused/pallas_call | solution.py:694
  47.7 1.4 %copy.18 = bf16[2,1,8192]{2,0,1:T(2,128)(2,1)} copy(bf16[2,1,8192]{2,0,1:T(2,128)(2,1)} %bitcast.16) | data formatting | bytes 65536
  (2 shorter events, 0.0 us)

commit v2 on v1

--- a/solution.py
+++ b/solution.py
@@ -184,15 +184,16 @@
 
 def fused_kernel(
     share, pool_here,
-    length_ref, turn_cos_ref, turn_sin_ref, query_ref, new_key_ref, new_value_ref,
-    chosen_ref, slot_ref, right_ref, coarse_cos_ref, coarse_sin_ref, fine_cos_ref, fine_sin_ref,
-    spread_ref, left_hbm, regroup_hbm, pool_hbm,
+    length_ref, pick_ref, turn_cos_ref, turn_sin_ref, query_ref, new_key_ref, new_value_ref,
+    chosen_ref, slot_ref, right_hbm, table_hbm, expand_hbm, spread_hbm, regroup_hbm, left_hbm,
+    pool_hbm,
     out_ref,
-    left_ref, regroup_ref, pool_ref, send_ref, ask_ref, asked_ref, row_ref,
-    place_ref, sign_ref, rotated_ref, fresh_key_ref, fresh_value_ref, flip_ref, token_ref,
-    cosine_ref, sine_ref, score_ref, fresh_ref, routed_ref, wire_ref, got_ref,
+    left_ref, right_ref, expand_ref, spread_ref, regroup_ref, pool_ref, block_ref,
+    send_ref, ask_ref, asked_ref, row_ref, place_ref, sign_ref, bound_ref,
+    rotated_ref, fresh_score_ref, fresh_value_ref, factor_ref, score_ref, fresh_ref,
+    routed_ref, wire_ref, got_ref,
     core_out, core_in, side_out, side_in, line_out, line_in, keep_ref,
-    left_sem, regroup_sem, pool_sem, row_sem, ask_send, ask_recv, wire_send, wire_recv,
+    in_sem, pool_sem, row_sem, ask_send, ask_recv, wire_send, wire_recv,
     core_send, core_recv, side_send, side_recv, line_send, line_recv,
 ):
     me = lax.axis_index("store")
@@ -201,7 +202,8 @@
     rows, picks = chosen_ref.shape
     heads, blocks = slot_ref.shape
     steps = rows // heads
-    rank = right_ref.shape[0]
+    rank = left_hbm.shape[0]
+    deep = left_ref.shape[0]
     group = query_ref.shape[1] // HEAD_SIZE // heads
     both = steps * group
     half = HEAD_SIZE // 2
@@ -234,10 +236,21 @@
 
     lax.fori_loop(1, holders, greet, 0)
 
-    left_copy = pltpu.make_async_copy(left_hbm, left_ref, left_sem.at[0])
-    regroup_copy = pltpu.make_async_copy(regroup_hbm, regroup_ref, regroup_sem.at[0])
-    left_copy.start()
-    regroup_copy.start()
+    loads = [
+        pltpu.make_async_copy(src, dst, in_sem.at[at])
+        for at, (src, dst) in enumerate(
+            (
+                (left_hbm, left_ref.at[pl.ds(0, rank)]),
+                (right_hbm, right_ref),
+                (table_hbm, block_ref.at[:, :, pl.ds(deep, 2 * HEAD_SIZE)]),
+                (expand_hbm, expand_ref),
+                (regroup_hbm, regroup_ref),
+                (spread_hbm, spread_ref),
+            )
+        )
+    ]
+    for copy in loads:
+        copy.start()
     octets = pool_here // 8
     pool_copies = [
         pltpu.make_async_copy(
@@ -252,52 +265,58 @@
         copy.start()
 
     total = holders * share
-    block_at = lax.broadcasted_iota(jnp.int32, (rows, blocks), 1)
-    chosen = chosen_ref[...]
-    hit = jnp.zeros((rows, blocks), jnp.int32)
-    for pick in range(picks):
-        hit = jnp.where(chosen[:, pick : pick + 1] == block_at, 1, hit)
-    slot = slot_ref[...]
+    length = length_ref[0]
+    lane_at = lax.broadcasted_iota(jnp.int32, (heads, total), 1)
+    first_step = lane_at < picks
+    chosen = jnp.concatenate([chosen_ref[s * heads : (s + 1) * heads] for s in range(steps)], 1)
+    slot = jnp.zeros((heads, total), jnp.int32)
+    for at in range(0, blocks, total):
+        found = jnp.take_along_axis(slot_ref[:, at : at + total], chosen & (total - 1), axis=1)
+        slot = jnp.where(chosen // total == at // total, found, slot)
     if pool_here & (pool_here - 1) == 0:
-        keeper_head = slot >> (pool_here.bit_length() - 1)
+        keeper = slot >> (pool_here.bit_length() - 1)
         inside = slot & (pool_here - 1)
     else:
-        keeper_head = lax.div(slot, jnp.full_like(slot, pool_here))
-        inside = slot - keeper_head * pool_here
+        keeper = lax.div(slot, jnp.full_like(slot, pool_here))
+        inside = slot - keeper * pool_here
     sign_ref[...] = (1 - 2 * (inside & 1)).astype(jnp.float32)
     inside = ((inside >> 1) & 3) * octets + (inside >> 3)
-    keeper = jnp.concatenate([keeper_head] * steps, 0)
-    kept = jnp.where(hit == 1, keeper, -1)
-    before = (
-        lax.broadcasted_iota(jnp.int32, (blocks, blocks), 0)
-        < lax.broadcasted_iota(jnp.int32, (blocks, blocks), 1)
-    ).astype(jnp.float32).astype(jnp.bfloat16)
-    mine = [jnp.where(kept == holder, 1.0, 0.0) for holder in range(holders)]
+    before_row = lax.broadcasted_iota(jnp.int32, (total, total), 0)
+    before_lane = lax.broadcasted_iota(jnp.int32, (total, total), 1)
+    before = jnp.where(
+        jnp.logical_and(before_row < before_lane, before_row // picks == before_lane // picks),
+        1.0, 0.0,
+    ).astype(jnp.bfloat16)
+    mine = [jnp.where(keeper == holder, 1.0, 0.0) for holder in range(holders)]
     counts = jnp.dot(
         jnp.concatenate(mine, 0).astype(jnp.bfloat16), before, preferred_element_type=jnp.float32
     )
-    order = jnp.zeros((rows, blocks), jnp.float32)
+    order = jnp.zeros((heads, total), jnp.float32)
     for holder in range(holders):
-        order = order + mine[holder] * counts[holder * rows : (holder + 1) * rows]
-    place = jnp.where(hit == 1, keeper * share + order.astype(jnp.int32), -1)
+        order = order + mine[holder] * counts[holder * heads : (holder + 1) * heads]
+    place = keeper * share + order.astype(jnp.int32)
     place_ref[...] = place
-    low = (inside & 255).astype(jnp.float32)
-    middle = ((inside >> 8) & 255).astype(jnp.float32)
-    high = (inside >> 16).astype(jnp.float32)
-    slot_at = lax.broadcasted_iota(jnp.int32, (total, blocks), 0)
-    moved = []
-    for row in range(rows):
-        head = row % heads
-        digits = jnp.concatenate(
-            [low[head : head + 1], middle[head : head + 1], high[head : head + 1],
-             jnp.zeros((5, blocks), jnp.float32)], 0
+    digits = []
+    for s in range(steps):
+        for shift in (0, 8, 16):
+            digit = ((inside >> shift) & 255).astype(jnp.float32)
+            digits.append(jnp.where(first_step == (s == 0), digit, 0.0))
+    slot_at = before_row
+    moved = [None] * rows
+    for head in range(heads):
+        lines = jnp.concatenate(
+            [digit[head : head + 1] for digit in digits]
+            + [jnp.zeros((8 - len(digits), total), jnp.float32)], 0
         ).astype(jnp.bfloat16)
-        table = jnp.where(place[row : row + 1] == slot_at, 1.0, 0.0).astype(jnp.bfloat16)
+        table = jnp.where(place[head : head + 1] == slot_at, 1.0, 0.0).astype(jnp.bfloat16)
         found = lax.dot_general(
-            digits, table, (((1,), (1,)), ((), ())), preferred_element_type=jnp.float32
+            lines, table, (((1,), (1,)), ((), ())), preferred_element_type=jnp.float32
         ).astype(jnp.int32)
-        found = found[0:1] + found[1:2] * 256 + found[2:3] * 65536
-        moved.append(pltpu.roll(found, row * share, 1) if row else found)
+        for s in range(steps):
+            row = s * heads + head
+            whole = found[3 * s : 3 * s + 1] + found[3 * s + 1 : 3 * s + 2] * 256
+            whole = whole + found[3 * s + 2 : 3 * s + 3] * 65536
+            moved[row] = pltpu.roll(whole, row * share, 1) if row else whole
     moved = jnp.concatenate(moved, 0)
     own_lanes = (
         lax.broadcasted_iota(jnp.int32, (rows, total), 1) // share
@@ -342,6 +361,10 @@
     both_cos = jnp.concatenate(spin_cos, 0)
     both_sin = jnp.concatenate(spin_sin, 0)
     empty = jnp.zeros((8 - steps, HEAD_SIZE), jnp.float32)
+    fresh_keep = (
+        lax.broadcasted_iota(jnp.int32, (both, 8), 1)
+        <= lax.broadcasted_iota(jnp.int32, (both, 8), 0) // group
+    )
     for head in range(heads):
         lanes = slice(head * HEAD_SIZE, (head + 1) * HEAD_SIZE)
         flat = jnp.concatenate(
@@ -352,118 +375,126 @@
             ],
             0,
         )
-        rotated_ref[head] = (
-            flat * both_cos + pltpu.roll(flat, half, 1) * both_sin
-        ).astype(jnp.bfloat16)
+        query = (flat * both_cos + pltpu.roll(flat, half, 1) * both_sin).astype(jnp.bfloat16)
+        for s in range(steps):
+            rotated_ref[s * heads + head] = query[s * group : (s + 1) * group]
         flat = jnp.concatenate([key_all[:, lanes], empty], 0)
-        fresh_key_ref[head] = (
-            flat * fresh_cos + pltpu.roll(flat, half, 1) * fresh_sin
-        ).astype(jnp.bfloat16)
+        fresh_key = (flat * fresh_cos + pltpu.roll(flat, half, 1) * fresh_sin).astype(jnp.bfloat16)
+        fresh = lax.dot_general(
+            query, fresh_key, (((1,), (1,)), ((), ())), preferred_element_type=jnp.float32
+        ) * scale
+        fresh_score_ref[head] = jnp.where(fresh_keep, fresh, -jnp.inf)
         fresh_value_ref[head] = jnp.concatenate([value_all[:, lanes], empty], 0).astype(
             jnp.bfloat16
         )
-        flip_ref[lanes, :] = right_ref[:, lanes].astype(jnp.float32).T.astype(jnp.bfloat16)
-    for t in range(BLOCK_TOKENS):
-        fine_cos, fine_sin = fine_cos_ref[t], fine_sin_ref[t]
-        cosine_ref[t] = coarse_cos_ref[...] * fine_cos - coarse_sin_ref[...] * fine_sin
-        sine_ref[t] = coarse_sin_ref[...] * fine_cos + coarse_cos_ref[...] * fine_sin
-    left_copy.wait()
-    regroup_copy.wait()
-    wide = regroup_ref.shape[0]
-    low_half = lax.broadcasted_iota(jnp.int32, (rank, 128), 1) < 64
-    for m in range(blocks // 128):
-        grouped = [
-            jnp.dot(
-                left_ref[:, (2 * m + n) * wide : (2 * m + n + 1) * wide], regroup_ref[...],
+    left_ref[rank:, :] = jnp.zeros((deep - rank, left_ref.shape[1]), jnp.bfloat16)
+    factor_ref[:, rank:, :] = jnp.zeros((heads, deep - rank, HEAD_SIZE), jnp.bfloat16)
+    loads[1].wait()
+    for head in range(heads):
+        factor_ref[head, :rank, :] = right_ref[:, head * HEAD_SIZE : (head + 1) * HEAD_SIZE]
+    loads[3].wait()
+    remaining = jnp.clip(length - chosen * BLOCK_TOKENS, 0, BLOCK_TOKENS)
+    bound_ref[...] = jnp.dot(
+        remaining.astype(jnp.float32).astype(jnp.bfloat16), expand_ref[...],
+        preferred_element_type=jnp.float32,
+    )
+    same = jnp.where(
+        lax.broadcasted_iota(jnp.int32, (deep, deep), 0)
+        == lax.broadcasted_iota(jnp.int32, (deep, deep), 1),
+        1.0, 0.0,
+    ).astype(jnp.bfloat16)
+    loads[0].wait()
+    turned_blocks = deep // BLOCK_TOKENS
+    for at in range(0, left_ref.shape[1], deep):
+        turned = lax.dot_general(
+            same, left_ref[:, at : at + deep], (((1,), (1,)), ((), ())),
+            preferred_element_type=jnp.float32,
+        )
+        first = at // BLOCK_TOKENS
+        block_ref[first : first + turned_blocks, :, :deep] = turned.reshape(
+            turned_blocks, BLOCK_TOKENS, deep
+        )
+    loads[2].wait()
+
+    token_at = (
+        lax.broadcasted_iota(jnp.int32, (group, picks * BLOCK_TOKENS), 1) % BLOCK_TOKENS
+    ).astype(jnp.float32)
+    low_half = lax.broadcasted_iota(jnp.int32, (group, total), 1) < picks
+
+    def one_row(row):
+        head = row // steps
+        s = row - head * steps
+        at = s * heads + head
+        found = [block_ref[pick_ref[at, pick]] for pick in range(picks)]
+        raw = jnp.dot(
+            jnp.concatenate([value[:, :deep] for value in found], 0).astype(jnp.bfloat16),
+            factor_ref[head], preferred_element_type=jnp.float32,
+        )
+        cosine = jnp.concatenate([value[:, deep : deep + HEAD_SIZE] for value in found], 0)
+        sine = jnp.concatenate([value[:, deep + HEAD_SIZE :] for value in found], 0)
+        keys = (raw * cosine + pltpu.roll(raw, half, 1) * sine).astype(jnp.bfloat16)
+        score_ref[row] = lax.dot_general(
+            rotated_ref[at], keys, (((1,), (1,)), ((), ())), preferred_element_type=jnp.float32
+        )
+
+    def key_rows(at, _):
+        for n in range(2):
+            one_row(at * 2 + n)
+        return 0
+
+    def weigh(part):
+        weights = []
+        for head in range(part * quad, (part + 1) * quad):
+            fresh_weights = []
+            for s in range(steps):
+                bound = jnp.broadcast_to(
+                    bound_ref[head : head + 1, s * picks * BLOCK_TOKENS : (s + 1) * picks * BLOCK_TOKENS],
+                    token_at.shape,
+                )
+                scores = jnp.where(token_at < bound, score_ref[head * steps + s] * scale, -jnp.inf)
+                fresh = fresh_score_ref[head, s * group : (s + 1) * group]
+                highest = jnp.maximum(
+                    jnp.max(scores, -1, keepdims=True), jnp.max(fresh, -1, keepdims=True)
+                )
+                power = jnp.exp(scores - highest)
+                fresh_power = jnp.exp(fresh - highest)
+                inverse = 1.0 / (
+                    jnp.sum(power, -1, keepdims=True) + jnp.sum(fresh_power, -1, keepdims=True)
+                )
+                weights.append(power * inverse)
+                fresh_weights.append(fresh_power * inverse)
+            fresh_ref[head * both : (head + 1) * both] = jnp.dot(
+                jnp.concatenate(fresh_weights, 0).astype(jnp.bfloat16), fresh_value_ref[head],
                 preferred_element_type=jnp.float32,
             )
-            for n in range(2)
-        ]
-        for t in range(0, BLOCK_TOKENS, 2):
-            a, b = (value[:, t * 64 : (t + 2) * 64] for value in grouped)
-            for odd, value in enumerate(
-                (
-                    jnp.where(low_half, a, pltpu.roll(b, 64, 1)),
-                    jnp.where(low_half, pltpu.roll(a, 64, 1), b),
-                )
-            ):
-                token_ref[t + odd, :, m * 128 : (m + 1) * 128] = value.astype(jnp.bfloat16)
-
-    length = length_ref[0]
-    place_at = lax.broadcasted_iota(jnp.int32, (total, blocks), 0)
-    first_token = lax.broadcasted_iota(jnp.int32, (both, blocks), 1) * BLOCK_TOKENS
-    fresh_keep = (
-        lax.broadcasted_iota(jnp.int32, (both, 8), 1)
-        <= lax.broadcasted_iota(jnp.int32, (both, 8), 0) // group
-    )
-    chunk = min(256, blocks)
-
-    def one_head(head, _):
-        query = rotated_ref[head]
-        factor = flip_ref[pl.ds(pl.multiple_of(head * HEAD_SIZE, HEAD_SIZE), HEAD_SIZE)]
-        for t in range(BLOCK_TOKENS):
-            for at in range(0, blocks, chunk):
-                lanes = slice(at, at + chunk)
-                raw = jnp.dot(
-                    factor, token_ref[t, :, lanes], preferred_element_type=jnp.float32
-                )
-                first, second = raw[:half], raw[half:]
-                cosine, sine = cosine_ref[t, :, lanes], sine_ref[t, :, lanes]
-                keys = jnp.concatenate(
-                    [first * cosine - second * sine, second * cosine + first * sine], 0
-                ).astype(jnp.bfloat16)
-                score_ref[t, :, lanes] = (
-                    jnp.dot(query, keys, preferred_element_type=jnp.float32) * scale
-                )
-        place = [place_ref[pl.ds(s * heads + head, 1)] for s in range(steps)]
-        place_rows = jnp.concatenate(
-            [jnp.broadcast_to(place[s], (group, blocks)) for s in range(steps)], 0
-        )
-        inside_at = jnp.where(place_rows >= 0, first_token, length)
-        scores = [
-            jnp.where(inside_at + t < length, score_ref[t], -jnp.inf)
-            for t in range(BLOCK_TOKENS)
-        ]
-        fresh = lax.dot_general(
-            query, fresh_key_ref[head], (((1,), (1,)), ((), ())),
+        grouped = jnp.dot(
+            jnp.concatenate(weights, 0).astype(jnp.bfloat16), regroup_ref[...],
             preferred_element_type=jnp.float32,
-        ) * scale
-        fresh = jnp.where(fresh_keep, fresh, -jnp.inf)
-        top = scores[0]
-        for t in range(1, BLOCK_TOKENS):
-            top = jnp.maximum(top, scores[t])
-        highest = jnp.maximum(
-            jnp.max(top, -1, keepdims=True), jnp.max(fresh, -1, keepdims=True)
-        )
-        powers = [jnp.exp(score - highest) for score in scores]
-        fresh_power = jnp.exp(fresh - highest)
-        whole = powers[0]
-        for t in range(1, BLOCK_TOKENS):
-            whole = whole + powers[t]
-        denominator = jnp.sum(whole, -1, keepdims=True) + jnp.sum(
-            fresh_power, -1, keepdims=True
-        )
-        inverse = 1.0 / denominator
-        fresh_ref[pl.ds(pl.multiple_of(head * both, both), both)] = jnp.dot(
-            (fresh_power * inverse).astype(jnp.bfloat16), fresh_value_ref[head],
-            preferred_element_type=jnp.float32,
-        )
-        sign = sign_ref[pl.ds(head, 1)]
-        for s in range(steps):
+        )
+        for h in range(quad):
+            head = part * quad + h
+            lines = []
+            for s in range(steps):
+                line = grouped[(h * steps + s) * group : (h * steps + s + 1) * group]
+                for t in range(BLOCK_TOKENS):
+                    value = line[:, t // 2 * total : (t // 2 + 1) * total]
+                    if t % 2 != s:
+                        value = pltpu.roll(value, picks, 1)
+                    lines.append(
+                        jnp.where(low_half, value, 0.0) if s == 0 else jnp.where(low_half, 0.0, value)
+                    )
             table = jnp.where(
-                place[s] == place_at, jnp.broadcast_to(sign, (total, blocks)), 0.0
-            ).astype(jnp.bfloat16)
-            stacked = jnp.concatenate(
-                [(power * inverse)[s * group : (s + 1) * group] for power in powers], 0
+                place_ref[head : head + 1] == slot_at,
+                jnp.broadcast_to(sign_ref[head : head + 1], (total, total)), 0.0,
             ).astype(jnp.bfloat16)
             routed = lax.dot_general(
-                stacked, table, (((1,), (1,)), ((), ())), preferred_element_type=jnp.float32
+                jnp.concatenate(lines, 0).astype(jnp.bfloat16), table, (((1,), (1,)), ((), ())),
+                preferred_element_type=jnp.float32,
             )
-            for t in range(BLOCK_TOKENS):
-                routed_ref[t, head, s * group : (s + 1) * group] = routed[
-                    t * group : (t + 1) * group
-                ]
-        return 0
+            for s in range(steps):
+                for t in range(BLOCK_TOKENS):
+                    at = (s * BLOCK_TOKENS + t) * group
+                    routed_ref[t, h, s * group : (s + 1) * group] = routed[at : at + group]
 
     lane = lax.broadcasted_iota(jnp.int32, (both, total), 1) // share
     middle_t = BLOCK_TOKENS // 2
@@ -475,11 +506,15 @@
             wire_send.at[part * holders + j], wire_recv.at[part * holders + j], target,
         )
 
+    loads[4].wait()
     for part in range(2):
-        lax.fori_loop(part * quad, (part + 1) * quad, one_head, 0)
+        lax.fori_loop(part * quad * steps // 2, (part + 1) * quad * steps // 2, key_rows, 0)
+        weigh(part)
+        if part == 0:
+            loads[5].wait()
         for upper in range(2):
             cells = [
-                routed_ref[upper * middle_t + t, part * quad + h]
+                routed_ref[upper * middle_t + t, h]
                 for t in range(middle_t)
                 for h in range(quad)
             ]
@@ -671,10 +706,12 @@
     inverse = ROPE_BASE ** (-(jnp.arange(half, dtype=jnp.float32) * 2.0 / HEAD_SIZE))
     angles = (lengths[0] + jnp.arange(steps, dtype=jnp.int32)).astype(jnp.float32)[:, None] * inverse
 
-    inverse = ROPE_BASE ** (-(np.arange(half, dtype=np.float32) * 2.0 / HEAD_SIZE))
-    coarse = inverse[:, None] * (np.arange(blocks) * BLOCK_TOKENS)[None, :]
-    fine = (np.arange(BLOCK_TOKENS)[:, None] * inverse[None, :])[..., None]
-    constant = lambda table: jnp.asarray(table.astype(np.float32))
+    turns = np.arange(tokens)[:, None] * ROPE_BASE ** (-(np.arange(half) * 2.0 / HEAD_SIZE))[None]
+    cosine, sine = np.cos(turns), np.sin(turns)
+    table = np.concatenate([cosine, cosine, -sine, sine], 1).astype(np.float32)
+    table = jnp.asarray(table.reshape(blocks, BLOCK_TOKENS, 2 * HEAD_SIZE))
+    expand = np.repeat(np.eye(steps * picks, dtype=np.float32), BLOCK_TOKENS, 1)
+    deep = -(-rank // 128) * 128
     wide = BLOCK_TOKENS * 64
     regroup = np.zeros((wide, wide), np.float32)
     for t in range(BLOCK_TOKENS):
@@ -693,29 +730,31 @@
     dma = pltpu.SemaphoreType.DMA
     attended = pl.pallas_call(
         functools.partial(fused_kernel, share, pool_here),
-        in_specs=[pl.BlockSpec(memory_space=pltpu.SMEM)] + [vmem] * 13 + [anywhere] * 3,
+        in_specs=[pl.BlockSpec(memory_space=pltpu.SMEM)] * 2 + [vmem] * 7 + [anywhere] * 7,
         out_specs=vmem,
         out_shape=jax.ShapeDtypeStruct((steps, heads * group * HEAD_SIZE), bf16),
         scratch_shapes=[
-            pltpu.VMEM((rank, tokens), bf16),
+            pltpu.VMEM((deep, tokens), bf16),
+            pltpu.VMEM((rank, heads * HEAD_SIZE), bf16),
+            pltpu.VMEM((steps * picks, steps * picks * BLOCK_TOKENS), bf16),
+            pltpu.VMEM((lines, 2 * lines), bf16),
             pltpu.VMEM((wide, wide), bf16),
             pltpu.VMEM((pool_here // 2, 2 * BLOCK_TOKENS, HEAD_SIZE), bf16),
+            pltpu.VMEM((blocks, BLOCK_TOKENS, deep + 2 * HEAD_SIZE), f32),
             pltpu.VMEM((holders, 1, slots), jnp.int32),
             pltpu.VMEM((holders, 1, slots), jnp.int32),
             pltpu.VMEM((holders, 1, slots), jnp.int32),
             pltpu.SMEM((holders, 1, slots), jnp.int32),
-            pltpu.VMEM((steps * heads, blocks), jnp.int32),
-            pltpu.VMEM((heads, blocks), f32),
-            pltpu.VMEM((heads, both, HEAD_SIZE), bf16),
+            pltpu.VMEM((heads, steps * picks), jnp.int32),
+            pltpu.VMEM((heads, steps * picks), f32),
+            pltpu.VMEM((heads, steps * picks * BLOCK_TOKENS), f32),
+            pltpu.VMEM((steps * heads, group, HEAD_SIZE), bf16),
+            pltpu.VMEM((heads, both, 8), f32),
             pltpu.VMEM((heads, 8, HEAD_SIZE), bf16),
-            pltpu.VMEM((heads, 8, HEAD_SIZE), bf16),
-            pltpu.VMEM((heads * HEAD_SIZE, rank), bf16),
-            pltpu.VMEM((BLOCK_TOKENS, rank, blocks), bf16),
-            pltpu.VMEM((BLOCK_TOKENS, half, blocks), f32),
-            pltpu.VMEM((BLOCK_TOKENS, half, blocks), f32),
-            pltpu.VMEM((BLOCK_TOKENS, both, blocks), f32),
+            pltpu.VMEM((heads, deep, HEAD_SIZE), bf16),
+            pltpu.VMEM((heads * steps, group, picks * BLOCK_TOKENS), f32),
             pltpu.VMEM((rows, HEAD_SIZE), f32),
-            pltpu.VMEM((BLOCK_TOKENS, heads, both, holders * share), f32),
+            pltpu.VMEM((BLOCK_TOKENS, quad, both, holders * share), f32),
             pltpu.VMEM((2, holders, both, lines), bf16),
             pltpu.VMEM((2, holders, both, lines), bf16),
             pltpu.VMEM((4, depth * piece, HEAD_SIZE), f32),
@@ -725,18 +764,18 @@
             pltpu.VMEM((2 * depth, piece, HEAD_SIZE), bf16),
             pltpu.VMEM((2 * depth, piece, HEAD_SIZE), bf16),
             pltpu.VMEM((rows, HEAD_SIZE), f32),
-            dma((1,)), dma((1,)), dma((4 * BLOCK_TOKENS,)), dma((1,)),
+            dma((6,)), dma((4 * BLOCK_TOKENS,)), dma((1,)),
             dma((holders,)), dma((holders,)), dma((2 * holders,)), dma((2 * holders,)),
             dma((4,)), dma((4,)), dma((2,)), dma((2,)), dma((2 * depth,)), dma((2 * depth,)),
         ],
         compiler_params=pltpu.CompilerParams(collective_id=0, has_side_effects=True),
         name="fused",
     )(
-        lengths, jnp.cos(angles), jnp.sin(angles), queries[:, 0], new_keys[:, 0],
-        incoming_values[:, 0], chosen[:, 0].reshape(steps * heads, picks), slot_map[0],
-        right_key_factor[0], constant(np.cos(coarse)), constant(np.sin(coarse)),
-        constant(np.cos(fine)), constant(np.sin(fine)), jnp.asarray(spread, bf16),
-        key_left[0].T, jnp.asarray(regroup, bf16),
+        lengths, chosen[:, 0].reshape(steps * heads, picks), jnp.cos(angles), jnp.sin(angles),
+        queries[:, 0], new_keys[:, 0], incoming_values[:, 0],
+        chosen[:, 0].reshape(steps * heads, picks), slot_map[0],
+        right_key_factor[0], table, jnp.asarray(expand, bf16), jnp.asarray(spread, bf16),
+        jnp.asarray(regroup, bf16), key_left[0].T,
         value_tile_store.reshape(pool_here // 8, 8, -1),
     )
     return attended.reshape(steps, 1, -1)
@@ -761,7 +800,8 @@
         blocks = args[6].shape[2]
         share = max(1, blocks // holders // 4)
         square = args[7].shape[0] * args[7].shape[2] == holders
-        fits = square and share == 8 and holders == 16 and blocks % 128 == 0
+        packed = args[7].shape[0] * args[7].shape[3] == holders * share
+        fits = square and packed and share == 8 and holders == 16 and blocks % 128 == 0
         return (fused_device if fits else per_device)(*args)
 
     return jax.shard_map(

time: 49.3 us -> 39.5 us (0.80)
  Pallas kernels: 46.3 us -> 36.5 us
    pallas_call x1, Pallas kernels: 46.3 us -> 36.5 us  [fused_device(): pl.pallas_call(functools.partial(fused_kernel, share, pool_here), in_spec...]
where the time goes in v2:
time: 39.5 us; the launch traced here: 39.3 us
  Pallas kernels  36.5 us (92%)
  local copies, waits for them, and re-layouts  1.4 us (4%)
  other arithmetic  0.71 us (2%)
  between operations  0.67 us (2%)
    pallas_call x1, Pallas kernels, fused_device(): pl.pallas_call(functools.partial(fused_kernel, share, pool_here), in_spec...  36.5 us
    unnamed x1, local copies, waits for them, and re-layouts  1.4 us

profile of v2, /device:TPU:0, one launch (start us, length us, event | category | flops | bytes accessed | tf_op | source)
XLA Modules:
  0.0 39.3 jit_solution(2415847302523539702)
XLA Ops:
  0.7 0.7 %multiply_sine_fusion = (f32[2,64]{1,0:T(2,128)}, f32[2,64]{1,0:T(2,128)}) fusion(f32[64]{0:T(128)S(1)} %negate_power_fusion, f32[2]{0:T(128)S(1)} %add_convert_fusion), kind=kLoop, calls=%fused_computation | loop fusion | flops 128 | bytes 1288 | tf_op jit(solution)/shard_map/sin | solution.py:774
  1.4 36.5 %fused.1 = bf16[2,8192]{1,0:T(2,128)(2,1)} custom-call(s32[1]{0:T(128)} %copy.15.length_ref, s32[16,64]{1,0:T(8,128)} %bitcast.18, f32[2,64]{1,0:T(2,128)} %get-tuple-element.6.turn_cos_ref, f32[2,64]{1,0:T(2,128)} %get-tuple-element.5.turn_sin_ref, bf16[2,8192]{1,0:T(2,128)(2,1)} %bitcast.17, bf16[2,1024]{1,0:T(2,128)(2,1)} %bitcast.21, ...), custom_call_target="tpu_custom_call" | custom-call | tf_op jit(solution)/shard_map/fused/pallas_call | solution.py:731
  37.9 1.4 %copy.16 = bf16[2,1,8192]{2,0,1:T(2,128)(2,1)} copy(bf16[2,1,8192]{2,0,1:T(2,128)(2,1)} %bitcast.16) | data formatting | bytes 65536
  (2 shorter events, 0.0 us)

commit v3 on v2

--- a/solution.py
+++ b/solution.py
@@ -184,19 +184,20 @@
 
 def fused_kernel(
     share, pool_here,
-    length_ref, pick_ref, turn_cos_ref, turn_sin_ref, query_ref, new_key_ref, new_value_ref,
+    length_ref, pick_ref, ahead_ref, query_ref, new_key_ref, new_value_ref,
     chosen_ref, slot_ref, right_hbm, table_hbm, expand_hbm, spread_hbm, regroup_hbm, left_hbm,
     pool_hbm,
     out_ref,
     left_ref, right_ref, expand_ref, spread_ref, regroup_ref, pool_ref, block_ref,
     send_ref, ask_ref, asked_ref, row_ref, place_ref, sign_ref, bound_ref,
-    rotated_ref, fresh_score_ref, fresh_value_ref, factor_ref, score_ref, fresh_ref,
+    rotated_ref, fresh_score_ref, fresh_value_ref, factor_ref, raw_even, raw_odd, turn_even, turn_odd, score_ref, fresh_ref,
     routed_ref, wire_ref, got_ref,
     core_out, core_in, side_out, side_in, line_out, line_in, keep_ref,
     in_sem, pool_sem, row_sem, ask_send, ask_recv, wire_send, wire_recv,
     core_send, core_recv, side_send, side_recv, line_send, line_recv,
 ):
     me = lax.axis_index("store")
+    raw_refs, turn_refs = (raw_even, raw_odd), (turn_even, turn_odd)
     holders = send_ref.shape[0]
     depth = holders // 4
     rows, picks = chosen_ref.shape
@@ -207,7 +208,8 @@
     group = query_ref.shape[1] // HEAD_SIZE // heads
     both = steps * group
     half = HEAD_SIZE // 2
-    quad = heads // 2
+    units = heads // 2
+    parts = ((0, units - 1), (units - 1, units))
     scale = HEAD_SIZE ** (-0.5)
     core, side, layer = lax.rem(me, 2), lax.rem(me // 2, 2), me // 4
 
@@ -261,8 +263,6 @@
         for q in range(4)
         for t in range(BLOCK_TOKENS)
     ]
-    for copy in pool_copies:
-        copy.start()
 
     total = holders * share
     length = length_ref[0]
@@ -340,19 +340,45 @@
         ask_copy(j).start()
     ask_ref[0] = send_ref[me]
 
-    spin_cos = [
-        jnp.broadcast_to(
-            jnp.concatenate([turn_cos_ref[s : s + 1]] * 2, 1), (group, HEAD_SIZE)
-        )
-        for s in range(steps)
-    ]
-    spin_sin = [
-        jnp.broadcast_to(
-            jnp.concatenate([-turn_sin_ref[s : s + 1], turn_sin_ref[s : s + 1]], 1),
-            (group, HEAD_SIZE),
-        )
-        for s in range(steps)
-    ]
+    left_ref[rank:, :] = jnp.zeros((deep - rank, left_ref.shape[1]), jnp.bfloat16)
+    factor_ref[:, rank:, :] = jnp.zeros((heads, deep - rank, HEAD_SIZE), jnp.bfloat16)
+    loads[1].wait()
+    for head in range(heads):
+        factor_ref[head, :rank, :] = right_ref[:, head * HEAD_SIZE : (head + 1) * HEAD_SIZE]
+    loads[3].wait()
+    remaining = jnp.clip(length - chosen * BLOCK_TOKENS, 0, BLOCK_TOKENS)
+    bound_ref[...] = jnp.dot(
+        remaining.astype(jnp.float32).astype(jnp.bfloat16), expand_ref[...],
+        preferred_element_type=jnp.float32,
+    )
+    same = jnp.where(before_row == before_lane, 1.0, 0.0).astype(jnp.bfloat16)
+    loads[0].wait()
+    turned_blocks = total // BLOCK_TOKENS
+    for at in range(0, left_ref.shape[1], total):
+        turned = lax.dot_general(
+            same, left_ref[:, at : at + total], (((1,), (1,)), ((), ())),
+            preferred_element_type=jnp.float32,
+        )
+        first = at // BLOCK_TOKENS
+        block_ref[first : first + turned_blocks, :, :deep] = turned.reshape(
+            turned_blocks, BLOCK_TOKENS, deep
+        )
+    loads[2].wait()
+    for copy in pool_copies:
+        copy.start()
+
+    last = jnp.maximum(length - 1, 0)
+    turn = block_ref[last // BLOCK_TOKENS, pl.ds(lax.rem(last, BLOCK_TOKENS), 1), deep:]
+    last_cos, last_sin = turn[:, :HEAD_SIZE], turn[:, HEAD_SIZE:]
+    spin_cos, spin_sin = [], []
+    for s in range(steps):
+        more_cos, more_sin = ahead_ref[2 * s : 2 * s + 1], ahead_ref[2 * s + 1 : 2 * s + 2]
+        spin_cos.append(
+            jnp.broadcast_to(last_cos * more_cos - last_sin * more_sin, (group, HEAD_SIZE))
+        )
+        spin_sin.append(
+            jnp.broadcast_to(last_sin * more_cos + last_cos * more_sin, (group, HEAD_SIZE))
+        )
     query_all = query_ref[...].astype(jnp.float32)
     key_all = new_key_ref[...].astype(jnp.float32)
     value_all = new_value_ref[...].astype(jnp.float32)
@@ -387,64 +413,49 @@
         fresh_value_ref[head] = jnp.concatenate([value_all[:, lanes], empty], 0).astype(
             jnp.bfloat16
         )
-    left_ref[rank:, :] = jnp.zeros((deep - rank, left_ref.shape[1]), jnp.bfloat16)
-    factor_ref[:, rank:, :] = jnp.zeros((heads, deep - rank, HEAD_SIZE), jnp.bfloat16)
-    loads[1].wait()
-    for head in range(heads):
-        factor_ref[head, :rank, :] = right_ref[:, head * HEAD_SIZE : (head + 1) * HEAD_SIZE]
-    loads[3].wait()
-    remaining = jnp.clip(length - chosen * BLOCK_TOKENS, 0, BLOCK_TOKENS)
-    bound_ref[...] = jnp.dot(
-        remaining.astype(jnp.float32).astype(jnp.bfloat16), expand_ref[...],
-        preferred_element_type=jnp.float32,
-    )
-    same = jnp.where(
-        lax.broadcasted_iota(jnp.int32, (deep, deep), 0)
-        == lax.broadcasted_iota(jnp.int32, (deep, deep), 1),
-        1.0, 0.0,
-    ).astype(jnp.bfloat16)
-    loads[0].wait()
-    turned_blocks = deep // BLOCK_TOKENS
-    for at in range(0, left_ref.shape[1], deep):
-        turned = lax.dot_general(
-            same, left_ref[:, at : at + deep], (((1,), (1,)), ((), ())),
-            preferred_element_type=jnp.float32,
-        )
-        first = at // BLOCK_TOKENS
-        block_ref[first : first + turned_blocks, :, :deep] = turned.reshape(
-            turned_blocks, BLOCK_TOKENS, deep
-        )
-    loads[2].wait()
 
     token_at = (
         lax.broadcasted_iota(jnp.int32, (group, picks * BLOCK_TOKENS), 1) % BLOCK_TOKENS
     ).astype(jnp.float32)
     low_half = lax.broadcasted_iota(jnp.int32, (group, total), 1) < picks
 
-    def one_row(row):
-        head = row // steps
-        s = row - head * steps
-        at = s * heads + head
-        found = [block_ref[pick_ref[at, pick]] for pick in range(picks)]
-        raw = jnp.dot(
+    portion = total // BLOCK_TOKENS
+    portions = picks // portion
+
+    def gather(row, at):
+        head, s = divmod(row, steps)
+        found = [
+            block_ref[pick_ref[s * heads + head, at * portion + n]] for n in range(portion)
+        ]
+        span = slice(at * total, (at + 1) * total)
+        raw_refs[row % 2][span] = jnp.dot(
             jnp.concatenate([value[:, :deep] for value in found], 0).astype(jnp.bfloat16),
             factor_ref[head], preferred_element_type=jnp.float32,
         )
-        cosine = jnp.concatenate([value[:, deep : deep + HEAD_SIZE] for value in found], 0)
-        sine = jnp.concatenate([value[:, deep + HEAD_SIZE :] for value in found], 0)
-        keys = (raw * cosine + pltpu.roll(raw, half, 1) * sine).astype(jnp.bfloat16)
-        score_ref[row] = lax.dot_general(
-            rotated_ref[at], keys, (((1,), (1,)), ((), ())), preferred_element_type=jnp.float32
-        )
-
-    def key_rows(at, _):
-        for n in range(2):
-            one_row(at * 2 + n)
-        return 0
+        turn_refs[row % 2][span] = jnp.concatenate([value[:, deep:] for value in found], 0)
+
+    def compare(row, at):
+        head, s = divmod(row, steps)
+        span = slice(at * total, (at + 1) * total)
+        raw = raw_refs[row % 2][span]
+        keys = raw * turn_refs[row % 2][span, :HEAD_SIZE]
+        keys = keys + pltpu.roll(raw, half, 1) * turn_refs[row % 2][span, HEAD_SIZE:]
+        score_ref[row, :, span] = lax.dot_general(
+            rotated_ref[s * heads + head], keys.astype(jnp.bfloat16), (((1,), (1,)), ((), ())),
+            preferred_element_type=jnp.float32,
+        )
+
+    def key_rows(first, last):
+        for row in range(first, last):
+            for at in range(portions):
+                if row + 1 < rows:
+                    gather(row + 1, at)
+                compare(row, at)
 
     def weigh(part):
         weights = []
-        for head in range(part * quad, (part + 1) * quad):
+        heads_here = range(2 * parts[part][0], 2 * parts[part][1])
+        for head in heads_here:
             fresh_weights = []
             for s in range(steps):
                 bound = jnp.broadcast_to(
@@ -471,8 +482,7 @@
             jnp.concatenate(weights, 0).astype(jnp.bfloat16), regroup_ref[...],
             preferred_element_type=jnp.float32,
         )
-        for h in range(quad):
-            head = part * quad + h
+        for h, head in enumerate(heads_here):
             lines = []
             for s in range(steps):
                 line = grouped[(h * steps + s) * group : (h * steps + s + 1) * group]
@@ -494,29 +504,28 @@
             for s in range(steps):
                 for t in range(BLOCK_TOKENS):
                     at = (s * BLOCK_TOKENS + t) * group
-                    routed_ref[t, h, s * group : (s + 1) * group] = routed[at : at + group]
+                    routed_ref[t, head, s * group : (s + 1) * group] = routed[at : at + group]
 
     lane = lax.broadcasted_iota(jnp.int32, (both, total), 1) // share
-    middle_t = BLOCK_TOKENS // 2
 
     def wire_copy(part, j):
         target = peer(j)
+        first, last = parts[part]
         return remote(
-            wire_ref.at[part, target], got_ref.at[part, j],
+            wire_ref.at[target, pl.ds(first, last - first)],
+            got_ref.at[j, pl.ds(first, last - first)],
             wire_send.at[part * holders + j], wire_recv.at[part * holders + j], target,
         )
 
     loads[4].wait()
-    for part in range(2):
-        lax.fori_loop(part * quad * steps // 2, (part + 1) * quad * steps // 2, key_rows, 0)
+    for at in range(portions):
+        gather(0, at)
+    for part, (first, last) in enumerate(parts):
+        key_rows(2 * first * steps, 2 * last * steps)
         weigh(part)
-        if part == 0:
-            loads[5].wait()
-        for upper in range(2):
+        for unit in range(first, last):
             cells = [
-                routed_ref[upper * middle_t + t, h]
-                for t in range(middle_t)
-                for h in range(quad)
+                routed_ref[t, 2 * unit + h] for t in range(BLOCK_TOKENS) for h in range(2)
             ]
             step = 1
             while step < holders:
@@ -534,12 +543,11 @@
                 cells = turned
                 step *= 2
             for holder in range(holders):
-                wire_ref[part, holder, :, upper * total : (upper + 1) * total] = cells[
-                    holder
-                ].astype(jnp.bfloat16)
+                wire_ref[holder, unit] = cells[holder].astype(jnp.bfloat16)
         for j in far_first:
             wire_copy(part, j).start()
 
+    loads[5].wait()
     for j in range(1, holders):
         ask_copy(j).wait_recv()
     asked_ref[...] = jnp.clip(ask_ref[...], 0, pool_ref.shape[0] - 1)
@@ -551,62 +559,60 @@
 
     early = lax.broadcasted_iota(jnp.int32, (both, HEAD_SIZE), 0) < group
 
-    def partial(part, j):
-        if j:
-            arrived = got_ref[part, j]
-        else:
-            arrived = wire_ref[part, me]
+    def partial(unit, j):
+        arrived = got_ref[j, unit] if j else wire_ref[me, unit]
         weight = jnp.maximum(
             jnp.dot(arrived, spread_ref[...], preferred_element_type=jnp.float32), 0.0
         )
-        results = []
-        for h in range(0, quad, 2):
-            lhs, columns = [], []
-            for h_at in (h, h + 1):
-                own = weight[:, h_at * HEAD_SIZE : (h_at + 1) * HEAD_SIZE]
-                lhs.append(
-                    jnp.concatenate(
-                        [jnp.where(early, own, 0.0), jnp.where(early, 0.0, own)], 1
-                    ).astype(jnp.bfloat16)
+        lhs, columns = [], []
+        for h in range(2):
+            own = weight[:, h * HEAD_SIZE : (h + 1) * HEAD_SIZE]
+            lhs.append(
+                jnp.concatenate(
+                    [jnp.where(early, own, 0.0), jnp.where(early, 0.0, own)], 1
+                ).astype(jnp.bfloat16)
+            )
+            columns.append(
+                jnp.concatenate(
+                    [
+                        pool_ref[row_ref[j, 0, (s * heads + 2 * unit + h) * share + n]]
+                        for s in range(steps)
+                        for n in range(share)
+                    ],
+                    0,
                 )
-                columns.append(
-                    jnp.concatenate(
-                        [
-                            pool_ref[
-                                row_ref[j, 0, (s * heads + part * quad + h_at) * share + n]
-                            ]
-                            for s in range(steps)
-                            for n in range(share)
-                        ],
-                        0,
-                    )
-                )
-            product = jnp.dot(
-                jnp.concatenate(lhs, 0), jnp.concatenate(columns, 1),
-                preferred_element_type=jnp.float32,
             )
-            results += [product[:both, :HEAD_SIZE], product[both:, HEAD_SIZE:]]
-        return jnp.concatenate(results, 0)
+        product = jnp.dot(
+            jnp.concatenate(lhs, 0), jnp.concatenate(columns, 1),
+            preferred_element_type=jnp.float32,
+        )
+        return jnp.concatenate([product[:both, :HEAD_SIZE], product[both:, HEAD_SIZE:]], 0)
 
     own_core = peer(2 * depth)
     own_side = peer(depth)
-    piece = quad * both
+
+    def span(part):
+        first, last = parts[part]
+        return pl.ds(first * 2 * both, (last - first) * 2 * both)
 
     def core_copy(part, across):
         at = part * 2 + across
         return remote(
-            core_out.at[at], core_in.at[at], core_send.at[at], core_recv.at[at], own_core
+            core_out.at[across, :, span(part)], core_in.at[across, :, span(part)],
+            core_send.at[at], core_recv.at[at], own_core,
         )
 
     def side_copy(part):
         return remote(
-            side_out.at[part], side_in.at[part], side_send.at[part], side_recv.at[part], own_side
+            side_out.at[:, span(part)], side_in.at[:, span(part)],
+            side_send.at[part], side_recv.at[part], own_side,
         )
 
     def line_copy(part, ahead):
         at = part * depth + ahead
         return remote(
-            line_out.at[at], line_in.at[at], line_send.at[at], line_recv.at[at],
+            line_out.at[ahead, span(part)], line_in.at[ahead, span(part)],
+            line_send.at[at], line_recv.at[at],
             lax.rem(layer - ahead + depth, depth) * 4 + side * 2 + core,
         )
 
@@ -616,50 +622,52 @@
         for j in js:
             if j:
                 wire_copy(part, j).wait_recv()
-        return [partial(part, j) for j in js]
+        return [
+            jnp.concatenate([partial(unit, j) for unit in range(*parts[part])], 0) for j in js
+        ]
 
     def far_stage(part, across):
         for ahead, value in enumerate(stage(part, 1, across)):
-            core_out[part * 2 + across, ahead * piece : (ahead + 1) * piece] = value
+            core_out[across, ahead, span(part)] = value
         core_copy(part, across).start()
 
     def side_stage(part):
         values = stage(part, 0, 1)
         core_copy(part, 1).wait_recv()
         for ahead, value in enumerate(values):
-            span = slice(ahead * piece, (ahead + 1) * piece)
-            side_out[part, span] = (value + core_in[part * 2 + 1, span]).astype(jnp.bfloat16)
+            side_out[ahead, span(part)] = (value + core_in[1, ahead, span(part)]).astype(
+                jnp.bfloat16
+            )
         side_copy(part).start()
 
     def line_stage(part):
         values = stage(part, 0, 0)
         core_copy(part, 0).wait_recv()
         side_copy(part).wait_recv()
-        for ahead, value in enumerate(values):
-            span = slice(ahead * piece, (ahead + 1) * piece)
-            value = value + core_in[part * 2, span] + side_in[part, span].astype(jnp.float32)
+        for ahead in list(range(1, depth)) + [0]:
+            value = values[ahead] + core_in[0, ahead, span(part)]
+            value = value + side_in[ahead, span(part)].astype(jnp.float32)
             if ahead:
-                line_out[part * depth + ahead] = value.astype(jnp.bfloat16)
+                line_out[ahead, span(part)] = value.astype(jnp.bfloat16)
                 line_copy(part, ahead).start()
             else:
-                keep_ref[part * piece : (part + 1) * piece] = value
+                keep_ref[span(part)] = value
 
     far_stage(0, 1)
     side_stage(0)
+    far_stage(1, 1)
+    side_stage(1)
     far_stage(0, 0)
-    far_stage(1, 1)
     line_stage(0)
-    side_stage(1)
     far_stage(1, 0)
     line_stage(1)
 
     for part in range(2):
-        span = slice(part * piece, (part + 1) * piece)
-        value = keep_ref[span] + fresh_ref[span]
+        value = keep_ref[span(part)] + fresh_ref[span(part)]
         for ahead in range(1, depth):
             line_copy(part, ahead).wait_recv()
-            value = value + line_in[part * depth + ahead].astype(jnp.float32)
-        keep_ref[span] = value
+            value = value + line_in[ahead, span(part)].astype(jnp.float32)
+        keep_ref[span(part)] = value
     for head in range(heads):
         for g in range(group):
             at = (head * group + g) * HEAD_SIZE
@@ -669,7 +677,7 @@
                     for s in range(steps)
                 ],
                 0,
-            ).astype(jnp.bfloat16)
+            )
 
     for j in range(1, holders):
         ask_copy(j).wait_send()
@@ -697,18 +705,15 @@
     slots = steps * heads * share
     rows = steps * heads * group
     both = steps * group
-    quad = heads // 2
+    units = heads // 2
     depth = holders // 4
-    piece = quad * both
     half = HEAD_SIZE // 2
     tokens = blocks * BLOCK_TOKENS
-
-    inverse = ROPE_BASE ** (-(jnp.arange(half, dtype=jnp.float32) * 2.0 / HEAD_SIZE))
-    angles = (lengths[0] + jnp.arange(steps, dtype=jnp.int32)).astype(jnp.float32)[:, None] * inverse
 
     turns = np.arange(tokens)[:, None] * ROPE_BASE ** (-(np.arange(half) * 2.0 / HEAD_SIZE))[None]
     cosine, sine = np.cos(turns), np.sin(turns)
     table = np.concatenate([cosine, cosine, -sine, sine], 1).astype(np.float32)
+    ahead = jnp.asarray(table[1 : steps + 1].reshape(2 * steps, HEAD_SIZE))
     table = jnp.asarray(table.reshape(blocks, BLOCK_TOKENS, 2 * HEAD_SIZE))
     expand = np.repeat(np.eye(steps * picks, dtype=np.float32), BLOCK_TOKENS, 1)
     deep = -(-rank // 128) * 128
@@ -716,12 +721,12 @@
     regroup = np.zeros((wide, wide), np.float32)
     for t in range(BLOCK_TOKENS):
         regroup[np.arange(64) * BLOCK_TOKENS + t, t * 64 + np.arange(64)] = 1.0
-    spread = np.zeros((BLOCK_TOKENS, quad, share, quad, share, BLOCK_TOKENS, 2), np.float32)
+    spread = np.zeros((BLOCK_TOKENS, 2, share, 2, share, BLOCK_TOKENS, 2), np.float32)
     for t in range(BLOCK_TOKENS):
-        for h in range(quad):
+        for h in range(2):
             for n in range(share):
                 spread[t, h, n, h, n, t] = (1.0, -1.0)
-    lines = BLOCK_TOKENS * quad * share
+    lines = BLOCK_TOKENS * 2 * share
     spread = spread.reshape(lines, 2 * lines)
 
     vmem = pl.BlockSpec(memory_space=pltpu.VMEM)
@@ -730,9 +735,9 @@
     dma = pltpu.SemaphoreType.DMA
     attended = pl.pallas_call(
         functools.partial(fused_kernel, share, pool_here),
-        in_specs=[pl.BlockSpec(memory_space=pltpu.SMEM)] * 2 + [vmem] * 7 + [anywhere] * 7,
+        in_specs=[pl.BlockSpec(memory_space=pltpu.SMEM)] * 2 + [vmem] * 6 + [anywhere] * 7,
         out_specs=vmem,
-        out_shape=jax.ShapeDtypeStruct((steps, heads * group * HEAD_SIZE), bf16),
+        out_shape=pltpu.VMEM((steps, heads * group * HEAD_SIZE), f32),
         scratch_shapes=[
             pltpu.VMEM((deep, tokens), bf16),
             pltpu.VMEM((rank, heads * HEAD_SIZE), bf16),
@@ -752,17 +757,21 @@
             pltpu.VMEM((heads, both, 8), f32),
             pltpu.VMEM((heads, 8, HEAD_SIZE), bf16),
             pltpu.VMEM((heads, deep, HEAD_SIZE), bf16),
+            pltpu.VMEM((picks * BLOCK_TOKENS, HEAD_SIZE), f32),
+            pltpu.VMEM((picks * BLOCK_TOKENS, HEAD_SIZE), f32),
+            pltpu.VMEM((picks * BLOCK_TOKENS, 2 * HEAD_SIZE), f32),
+            pltpu.VMEM((picks * BLOCK_TOKENS, 2 * HEAD_SIZE), f32),
             pltpu.VMEM((heads * steps, group, picks * BLOCK_TOKENS), f32),
             pltpu.VMEM((rows, HEAD_SIZE), f32),
-            pltpu.VMEM((BLOCK_TOKENS, quad, both, holders * share), f32),
-            pltpu.VMEM((2, holders, both, lines), bf16),
-            pltpu.VMEM((2, holders, both, lines), bf16),
-            pltpu.VMEM((4, depth * piece, HEAD_SIZE), f32),
-            pltpu.VMEM((4, depth * piece, HEAD_SIZE), f32),
-            pltpu.VMEM((2, depth * piece, HEAD_SIZE), bf16),
-            pltpu.VMEM((2, depth * piece, HEAD_SIZE), bf16),
-            pltpu.VMEM((2 * depth, piece, HEAD_SIZE), bf16),
-            pltpu.VMEM((2 * depth, piece, HEAD_SIZE), bf16),
+            pltpu.VMEM((BLOCK_TOKENS, heads, both, holders * share), f32),
+            pltpu.VMEM((holders, units, both, lines), bf16),
+            pltpu.VMEM((holders, units, both, lines), bf16),
+            pltpu.VMEM((2, depth, rows, HEAD_SIZE), f32),
+            pltpu.VMEM((2, depth, rows, HEAD_SIZE), f32),
+            pltpu.VMEM((depth, rows, HEAD_SIZE), bf16),
+            pltpu.VMEM((depth, rows, HEAD_SIZE), bf16),
+            pltpu.VMEM((depth, rows, HEAD_SIZE), bf16),
+            pltpu.VMEM((depth, rows, HEAD_SIZE), bf16),
             pltpu.VMEM((rows, HEAD_SIZE), f32),
             dma((6,)), dma((4 * BLOCK_TOKENS,)), dma((1,)),
             dma((holders,)), dma((holders,)), dma((2 * holders,)), dma((2 * holders,)),
@@ -771,14 +780,14 @@
         compiler_params=pltpu.CompilerParams(collective_id=0, has_side_effects=True),
         name="fused",
     )(
-        lengths, chosen[:, 0].reshape(steps * heads, picks), jnp.cos(angles), jnp.sin(angles),
+        lengths, chosen[:, 0].reshape(steps * heads, picks), ahead,
         queries[:, 0], new_keys[:, 0], incoming_values[:, 0],
         chosen[:, 0].reshape(steps * heads, picks), slot_map[0],
         right_key_factor[0], table, jnp.asarray(expand, bf16), jnp.asarray(spread, bf16),
         jnp.asarray(regroup, bf16), key_left[0].T,
         value_tile_store.reshape(pool_here // 8, 8, -1),
     )
-    return attended.reshape(steps, 1, -1)
+    return attended.astype(bf16).reshape(steps, 1, -1)
 
 
 def solution(mesh):

time: 39.5 us -> 31.9 us (0.81)
  Pallas kernels: 36.5 us -> 30.4 us
  local copies, waits for them, and re-layouts: 1.4 us -> 0 us
    pallas_call x1, Pallas kernels: 36.5 us -> 30.4 us  [fused_device(): pl.pallas_call(functools.partial(fused_kernel, share, pool_here), in_spec...]
    unnamed x1 -> x0, local copies, waits for them, and re-layouts: 1.4 us -> none
    sin x1 -> x0, other arithmetic: 0.69 us -> none  [fused_device(): jnp.sin(angles)]
    reshape x0 -> x1, other arithmetic: none -> 0.64 us  [fused_device(): return attended.astype(bf16).reshape(steps, 1, -1)]
where the time goes in v3:
time: 31.9 us; the launch traced here: 31.7 us
  Pallas kernels  30.4 us (95%)
  between operations  0.66 us (2%)
  other arithmetic  0.64 us (2%)
    pallas_call x1, Pallas kernels, fused_device(): pl.pallas_call(functools.partial(fused_kernel, share, pool_here), in_spec...  30.4 us
    reshape x1, other arithmetic, fused_device(): return attended.astype(bf16).reshape(steps, 1, -1)  0.64 us

profile of v3, /device:TPU:0, one launch (start us, length us, event | category | flops | bytes accessed | tf_op | source)
XLA Modules:
  0.0 31.7 jit_solution(11385768615783364068)
XLA Ops:
  0.7 30.4 %fused.1 = f32[2,8192]{1,0:T(2,128)S(1)} custom-call(s32[1]{0:T(128)S(6)} %copy.15.length_ref, s32[16,64]{1,0:T(8,128)} %bitcast.16, f32[4,128]{1,0:T(4,128)} %constant.10.clone.ahead_ref, bf16[2,8192]{1,0:T(2,128)(2,1)} %bitcast.15, bf16[2,1024]{1,0:T(2,128)(2,1)} %bitcast.19, bf16[2,1024]{1,0:T(2,128)(2,1)} %bitcast.20, s32[16,64]{1,0:T(8,128)} %bitcast.17, ...), custom_call_target="tpu_custom_call" | custom-call | tf_op jit(solution)/shard_map/fused/pallas_call | solution.py:736
  31.1 0.6 %convert_bitcast_fusion = bf16[2,1,8192]{2,0,1:T(2,128)(2,1)} fusion(f32[2,8192]{1,0:T(2,128)S(1)} %fused.1), kind=kLoop, calls=%fused_computation | loop fusion | flops 16384 | bytes 98304 | tf_op jit(solution)/shard_map/reshape | solution.py:790

commit v4 on v3

--- a/solution.py
+++ b/solution.py
@@ -209,7 +209,7 @@
     both = steps * group
     half = HEAD_SIZE // 2
     units = heads // 2
-    parts = ((0, units - 1), (units - 1, units))
+    parts = ((0, units - 2), (units - 2, units - 1), (units - 1, units))
     scale = HEAD_SIZE ** (-0.5)
     core, side, layer = lax.rem(me, 2), lax.rem(me // 2, 2), me // 4
 
@@ -258,7 +258,7 @@
         pltpu.make_async_copy(
             pool_hbm.at[:, pl.ds(2 * q, 2), pl.ds(HEAD_SIZE * t, HEAD_SIZE)],
             pool_ref.at[pl.ds(q * octets, octets), pl.ds(2 * t, 2), :],
-            pool_sem.at[q * BLOCK_TOKENS + t],
+            pool_sem.at[0],
         )
         for q in range(4)
         for t in range(BLOCK_TOKENS)
@@ -329,7 +329,7 @@
     def ask_copy(j):
         target = peer(j)
         return remote(
-            send_ref.at[target], ask_ref.at[j], ask_send.at[j], ask_recv.at[j], target
+            send_ref.at[target], ask_ref.at[j], ask_send.at[0], ask_recv.at[0], target
         )
 
     far_first = sorted(
@@ -341,10 +341,14 @@
     ask_ref[0] = send_ref[me]
 
     left_ref[rank:, :] = jnp.zeros((deep - rank, left_ref.shape[1]), jnp.bfloat16)
-    factor_ref[:, rank:, :] = jnp.zeros((heads, deep - rank, HEAD_SIZE), jnp.bfloat16)
+    factor_ref[:, rank:, :] = jnp.zeros((heads, deep - rank, 2 * HEAD_SIZE), jnp.bfloat16)
     loads[1].wait()
     for head in range(heads):
-        factor_ref[head, :rank, :] = right_ref[:, head * HEAD_SIZE : (head + 1) * HEAD_SIZE]
+        factor = right_ref[:, head * HEAD_SIZE : (head + 1) * HEAD_SIZE]
+        factor_ref[head, :rank, :HEAD_SIZE] = factor
+        factor_ref[head, :rank, HEAD_SIZE:] = pltpu.roll(
+            factor.astype(jnp.float32), half, 1
+        ).astype(jnp.bfloat16)
     loads[3].wait()
     remaining = jnp.clip(length - chosen * BLOCK_TOKENS, 0, BLOCK_TOKENS)
     bound_ref[...] = jnp.dot(
@@ -419,7 +423,7 @@
     ).astype(jnp.float32)
     low_half = lax.broadcasted_iota(jnp.int32, (group, total), 1) < picks
 
-    portion = total // BLOCK_TOKENS
+    portion = 2 * total // BLOCK_TOKENS
     portions = picks // portion
 
     def gather(row, at):
@@ -427,7 +431,7 @@
         found = [
             block_ref[pick_ref[s * heads + head, at * portion + n]] for n in range(portion)
         ]
-        span = slice(at * total, (at + 1) * total)
+        span = slice(2 * at * total, 2 * (at + 1) * total)
         raw_refs[row % 2][span] = jnp.dot(
             jnp.concatenate([value[:, :deep] for value in found], 0).astype(jnp.bfloat16),
             factor_ref[head], preferred_element_type=jnp.float32,
@@ -436,10 +440,10 @@
 
     def compare(row, at):
         head, s = divmod(row, steps)
-        span = slice(at * total, (at + 1) * total)
+        span = slice(2 * at * total, 2 * (at + 1) * total)
         raw = raw_refs[row % 2][span]
-        keys = raw * turn_refs[row % 2][span, :HEAD_SIZE]
-        keys = keys + pltpu.roll(raw, half, 1) * turn_refs[row % 2][span, HEAD_SIZE:]
+        keys = raw * turn_refs[row % 2][span]
+        keys = keys[:, :HEAD_SIZE] + keys[:, HEAD_SIZE:]
         score_ref[row, :, span] = lax.dot_general(
             rotated_ref[s * heads + head], keys.astype(jnp.bfloat16), (((1,), (1,)), ((), ())),
             preferred_element_type=jnp.float32,
@@ -514,7 +518,24 @@
         return remote(
             wire_ref.at[target, pl.ds(first, last - first)],
             got_ref.at[j, pl.ds(first, last - first)],
-            wire_send.at[part * holders + j], wire_recv.at[part * holders + j], target,
+            wire_send.at[part], wire_recv.at[part * 4 + j // depth], target,
+        )
+
+    def wires_in(part, quarter):
+        first, last = parts[part]
+        span = (pl.ds(max(1, quarter * depth), min(depth, quarter * depth + depth - 1)),
+                pl.ds(first, last - first))
+        return remote(
+            wire_ref.at[span], got_ref.at[span],
+            wire_send.at[part], wire_recv.at[part * 4 + quarter], peer(1),
+        )
+
+    def wires_out(part):
+        first, last = parts[part]
+        span = (pl.ds(1, holders - 1), pl.ds(first, last - first))
+        return remote(
+            wire_ref.at[span], got_ref.at[span],
+            wire_send.at[part], wire_recv.at[part * 4], peer(1),
         )
 
     loads[4].wait()
@@ -548,14 +569,16 @@
             wire_copy(part, j).start()
 
     loads[5].wait()
-    for j in range(1, holders):
-        ask_copy(j).wait_recv()
+    others = pl.ds(1, holders - 1)
+    all_asks = remote(
+        send_ref.at[others], ask_ref.at[others], ask_send.at[0], ask_recv.at[0], peer(1)
+    )
+    all_asks.wait_recv()
     asked_ref[...] = jnp.clip(ask_ref[...], 0, pool_ref.shape[0] - 1)
     row_copy = pltpu.make_async_copy(asked_ref, row_ref, row_sem.at[0])
     row_copy.start()
     row_copy.wait()
-    for copy in pool_copies:
-        copy.wait()
+    pltpu.make_async_copy(pool_ref, pool_ref, pool_sem.at[0]).wait()
 
     early = lax.broadcasted_iota(jnp.int32, (both, HEAD_SIZE), 0) < group
 
@@ -609,30 +632,32 @@
         )
 
     def line_copy(part, ahead):
-        at = part * depth + ahead
         return remote(
             line_out.at[ahead, span(part)], line_in.at[ahead, span(part)],
-            line_send.at[at], line_recv.at[at],
+            line_send.at[part], line_recv.at[part],
             lax.rem(layer - ahead + depth, depth) * 4 + side * 2 + core,
         )
 
-    def stage(part, far, across):
-        first = far * 2 * depth + across * depth
-        js = [first + ahead for ahead in range(depth)]
-        for j in js:
-            if j:
-                wire_copy(part, j).wait_recv()
-        return [
-            jnp.concatenate([partial(unit, j) for unit in range(*parts[part])], 0) for j in js
-        ]
+    def all_lines(part):
+        rest = (pl.ds(1, depth - 1), span(part))
+        return remote(
+            line_out.at[rest], line_in.at[rest], line_send.at[part], line_recv.at[part], peer(1)
+        )
+
+    def values_of(part, j):
+        return jnp.concatenate([partial(unit, j) for unit in range(*parts[part])], 0)
 
     def far_stage(part, across):
-        for ahead, value in enumerate(stage(part, 1, across)):
+        first = 2 * depth + across * depth
+        wires_in(part, 2 + across).wait_recv()
+        values = [values_of(part, first + ahead) for ahead in range(depth)]
+        for ahead, value in enumerate(values):
             core_out[across, ahead, span(part)] = value
         core_copy(part, across).start()
 
     def side_stage(part):
-        values = stage(part, 0, 1)
+        wires_in(part, 1).wait_recv()
+        values = [values_of(part, depth + ahead) for ahead in range(depth)]
         core_copy(part, 1).wait_recv()
         for ahead, value in enumerate(values):
             side_out[ahead, span(part)] = (value + core_in[1, ahead, span(part)]).astype(
@@ -641,31 +666,43 @@
         side_copy(part).start()
 
     def line_stage(part):
-        values = stage(part, 0, 0)
+        wires_in(part, 0).wait_recv()
+        values = [values_of(part, ahead) for ahead in range(1, depth)]
         core_copy(part, 0).wait_recv()
         side_copy(part).wait_recv()
-        for ahead in list(range(1, depth)) + [0]:
-            value = values[ahead] + core_in[0, ahead, span(part)]
+        for ahead in range(1, depth):
+            value = values[ahead - 1] + core_in[0, ahead, span(part)]
             value = value + side_in[ahead, span(part)].astype(jnp.float32)
-            if ahead:
-                line_out[ahead, span(part)] = value.astype(jnp.bfloat16)
-                line_copy(part, ahead).start()
-            else:
-                keep_ref[span(part)] = value
+            line_out[ahead, span(part)] = value.astype(jnp.bfloat16)
+        for ahead in range(1, depth):
+            line_copy(part, ahead).start()
 
     far_stage(0, 1)
     side_stage(0)
     far_stage(1, 1)
     side_stage(1)
     far_stage(0, 0)
+    far_stage(2, 1)
+    side_stage(2)
     line_stage(0)
     far_stage(1, 0)
     line_stage(1)
-
-    for part in range(2):
-        value = keep_ref[span(part)] + fresh_ref[span(part)]
+    far_stage(2, 0)
+    line_stage(2)
+
+    for part in range(len(parts)):
+        value = values_of(part, 0) + fresh_ref[span(part)] + core_in[0, 0, span(part)]
+        keep_ref[span(part)] = value + side_in[0, span(part)].astype(jnp.float32)
+    all_asks.wait_send()
+    for part in range(len(parts)):
+        wires_out(part).wait_send()
+        core_copy(part, 0).wait_send()
+        core_copy(part, 1).wait_send()
+        side_copy(part).wait_send()
+    for part in range(len(parts)):
+        all_lines(part).wait_recv()
+        value = keep_ref[span(part)]
         for ahead in range(1, depth):
-            line_copy(part, ahead).wait_recv()
             value = value + line_in[ahead, span(part)].astype(jnp.float32)
         keep_ref[span(part)] = value
     for head in range(heads):
@@ -679,16 +716,8 @@
                 0,
             )
 
-    for j in range(1, holders):
-        ask_copy(j).wait_send()
-        for part in range(2):
-            wire_copy(part, j).wait_send()
-    for part in range(2):
-        core_copy(part, 0).wait_send()
-        core_copy(part, 1).wait_send()
-        side_copy(part).wait_send()
-        for ahead in range(1, depth):
-            line_copy(part, ahead).wait_send()
+    for part in range(len(parts)):
+        all_lines(part).wait_send()
 
 
 def fused_device(
@@ -756,9 +785,9 @@
             pltpu.VMEM((steps * heads, group, HEAD_SIZE), bf16),
             pltpu.VMEM((heads, both, 8), f32),
             pltpu.VMEM((heads, 8, HEAD_SIZE), bf16),
-            pltpu.VMEM((heads, deep, HEAD_SIZE), bf16),
-            pltpu.VMEM((picks * BLOCK_TOKENS, HEAD_SIZE), f32),
-            pltpu.VMEM((picks * BLOCK_TOKENS, HEAD_SIZE), f32),
+            pltpu.VMEM((heads, deep, 2 * HEAD_SIZE), bf16),
+            pltpu.VMEM((picks * BLOCK_TOKENS, 2 * HEAD_SIZE), f32),
+            pltpu.VMEM((picks * BLOCK_TOKENS, 2 * HEAD_SIZE), f32),
             pltpu.VMEM((picks * BLOCK_TOKENS, 2 * HEAD_SIZE), f32),
             pltpu.VMEM((picks * BLOCK_TOKENS, 2 * HEAD_SIZE), f32),
             pltpu.VMEM((heads * steps, group, picks * BLOCK_TOKENS), f32),
@@ -773,9 +802,8 @@
             pltpu.VMEM((depth, rows, HEAD_SIZE), bf16),
             pltpu.VMEM((depth, rows, HEAD_SIZE), bf16),
             pltpu.VMEM((rows, HEAD_SIZE), f32),
-            dma((6,)), dma((4 * BLOCK_TOKENS,)), dma((1,)),
-            dma((holders,)), dma((holders,)), dma((2 * holders,)), dma((2 * holders,)),
-            dma((4,)), dma((4,)), dma((2,)), dma((2,)), dma((2 * depth,)), dma((2 * depth,)),
+            dma((6,)), dma((1,)), dma((1,)), dma((1,)), dma((1,)), dma((3,)), dma((12,)),
+            dma((6,)), dma((6,)), dma((3,)), dma((3,)), dma((3,)), dma((3,)),
         ],
         compiler_params=pltpu.CompilerParams(collective_id=0, has_side_effects=True),
         name="fused",

time: 31.9 us -> 29.8 us (0.934)
  Pallas kernels: 30.4 us -> 28.3 us
    pallas_call x1, Pallas kernels: 30.4 us -> 28.3 us  [fused_device(): pl.pallas_call(functools.partial(fused_kernel, share, pool_here), in_spec...]
where the time goes in v4:
time: 29.8 us; the launch traced here: 29.6 us
  Pallas kernels  28.3 us (95%)
  between operations  0.66 us (2%)
  other arithmetic  0.64 us (2%)
    pallas_call x1, Pallas kernels, fused_device(): pl.pallas_call(functools.partial(fused_kernel, share, pool_here), in_spec...  28.3 us
    reshape x1, other arithmetic, fused_device(): return attended.astype(bf16).reshape(steps, 1, -1)  0.64 us

profile of v4, /device:TPU:0, one launch (start us, length us, event | category | flops | bytes accessed | tf_op | source)
XLA Modules:
  0.0 29.6 jit_solution(4333690722162523714)
XLA Ops:
  0.7 28.3 %fused.1 = f32[2,8192]{1,0:T(2,128)S(1)} custom-call(s32[1]{0:T(128)S(6)} %copy.15.length_ref, s32[16,64]{1,0:T(8,128)} %bitcast.16, f32[4,128]{1,0:T(4,128)} %constant.10.clone.ahead_ref, bf16[2,8192]{1,0:T(2,128)(2,1)} %bitcast.15, bf16[2,1024]{1,0:T(2,128)(2,1)} %bitcast.19, bf16[2,1024]{1,0:T(2,128)(2,1)} %bitcast.20, s32[16,64]{1,0:T(8,128)} %bitcast.17, ...), custom_call_target="tpu_custom_call" | custom-call | tf_op jit(solution)/shard_map/fused/pallas_call | solution.py:765
  29.0 0.6 %convert_bitcast_fusion = bf16[2,1,8192]{2,0,1:T(2,128)(2,1)} fusion(f32[2,8192]{1,0:T(2,128)S(1)} %fused.1), kind=kLoop, calls=%fused_computation | loop fusion | flops 16384 | bytes 98304 | tf_op jit(solution)/shard_map/reshape | solution.py:818

commit v5 on v4

--- a/solution.py
+++ b/solution.py
@@ -204,7 +204,7 @@
     heads, blocks = slot_ref.shape
     steps = rows // heads
     rank = left_hbm.shape[0]
-    deep = left_ref.shape[0]
+    deep = block_ref.shape[2] - 2 * HEAD_SIZE
     group = query_ref.shape[1] // HEAD_SIZE // heads
     both = steps * group
     half = HEAD_SIZE // 2
@@ -242,7 +242,7 @@
         pltpu.make_async_copy(src, dst, in_sem.at[at])
         for at, (src, dst) in enumerate(
             (
-                (left_hbm, left_ref.at[pl.ds(0, rank)]),
+                (left_hbm, left_ref),
                 (right_hbm, right_ref),
                 (table_hbm, block_ref.at[:, :, pl.ds(deep, 2 * HEAD_SIZE)]),
                 (expand_hbm, expand_ref),
@@ -340,13 +340,11 @@
         ask_copy(j).start()
     ask_ref[0] = send_ref[me]
 
-    left_ref[rank:, :] = jnp.zeros((deep - rank, left_ref.shape[1]), jnp.bfloat16)
-    factor_ref[:, rank:, :] = jnp.zeros((heads, deep - rank, 2 * HEAD_SIZE), jnp.bfloat16)
     loads[1].wait()
     for head in range(heads):
         factor = right_ref[:, head * HEAD_SIZE : (head + 1) * HEAD_SIZE]
-        factor_ref[head, :rank, :HEAD_SIZE] = factor
-        factor_ref[head, :rank, HEAD_SIZE:] = pltpu.roll(
+        factor_ref[head, :, :HEAD_SIZE] = factor
+        factor_ref[head, :, HEAD_SIZE:] = pltpu.roll(
             factor.astype(jnp.float32), half, 1
         ).astype(jnp.bfloat16)
     loads[3].wait()
@@ -364,8 +362,8 @@
             preferred_element_type=jnp.float32,
         )
         first = at // BLOCK_TOKENS
-        block_ref[first : first + turned_blocks, :, :deep] = turned.reshape(
-            turned_blocks, BLOCK_TOKENS, deep
+        block_ref[first : first + turned_blocks, :, :rank] = turned.reshape(
+            turned_blocks, BLOCK_TOKENS, rank
         )
     loads[2].wait()
     for copy in pool_copies:
@@ -433,7 +431,7 @@
         ]
         span = slice(2 * at * total, 2 * (at + 1) * total)
         raw_refs[row % 2][span] = jnp.dot(
-            jnp.concatenate([value[:, :deep] for value in found], 0).astype(jnp.bfloat16),
+            jnp.concatenate([value[:, :rank] for value in found], 0).astype(jnp.bfloat16),
             factor_ref[head], preferred_element_type=jnp.float32,
         )
         turn_refs[row % 2][span] = jnp.concatenate([value[:, deep:] for value in found], 0)
@@ -482,6 +480,7 @@
                 jnp.concatenate(fresh_weights, 0).astype(jnp.bfloat16), fresh_value_ref[head],
                 preferred_element_type=jnp.float32,
             )
+        yield
         grouped = jnp.dot(
             jnp.concatenate(weights, 0).astype(jnp.bfloat16), regroup_ref[...],
             preferred_element_type=jnp.float32,
@@ -541,9 +540,7 @@
     loads[4].wait()
     for at in range(portions):
         gather(0, at)
-    for part, (first, last) in enumerate(parts):
-        key_rows(2 * first * steps, 2 * last * steps)
-        weigh(part)
+    def cross(first, last):
         for unit in range(first, last):
             cells = [
                 routed_ref[t, 2 * unit + h] for t in range(BLOCK_TOKENS) for h in range(2)
@@ -565,8 +562,23 @@
                 step *= 2
             for holder in range(holders):
                 wire_ref[holder, unit] = cells[holder].astype(jnp.bfloat16)
+    key_rows(0, 2 * parts[0][1] * steps)
+    for part, (first, last) in enumerate(parts):
+        later = [
+            (row, row + 1) for row in range(2 * last * steps, 2 * (last + 1) * steps) if row < rows
+        ]
+        for _ in weigh(part):
+            if later:
+                key_rows(*later.pop(0))
+        if later:
+            key_rows(*later.pop(0))
+        cross(first, last)
+        if later:
+            key_rows(*later.pop(0))
         for j in far_first:
             wire_copy(part, j).start()
+        for span_rows in later:
+            key_rows(*span_rows)
 
     loads[5].wait()
     others = pl.ds(1, holders - 1)
@@ -582,11 +594,20 @@
 
     early = lax.broadcasted_iota(jnp.int32, (both, HEAD_SIZE), 0) < group
 
-    def partial(unit, j):
-        arrived = got_ref[j, unit] if j else wire_ref[me, unit]
+    def partials(pieces):
+        arrived = [got_ref[j, unit] if j else wire_ref[me, unit] for unit, j in pieces]
         weight = jnp.maximum(
-            jnp.dot(arrived, spread_ref[...], preferred_element_type=jnp.float32), 0.0
-        )
+            jnp.dot(
+                jnp.concatenate(arrived, 0), spread_ref[...], preferred_element_type=jnp.float32
+            ),
+            0.0,
+        )
+        return [
+            partial(unit, j, weight[at * both : (at + 1) * both])
+            for at, (unit, j) in enumerate(pieces)
+        ]
+
+    def partial(unit, j, weight):
         lhs, columns = [], []
         for h in range(2):
             own = weight[:, h * HEAD_SIZE : (h + 1) * HEAD_SIZE]
@@ -644,20 +665,25 @@
             line_out.at[rest], line_in.at[rest], line_send.at[part], line_recv.at[part], peer(1)
         )
 
-    def values_of(part, j):
-        return jnp.concatenate([partial(unit, j) for unit in range(*parts[part])], 0)
+    def values_of(part, js):
+        units_here = range(*parts[part])
+        found = partials([(unit, j) for j in js for unit in units_here])
+        count = len(units_here)
+        return [
+            jnp.concatenate(found[at * count : (at + 1) * count], 0) for at in range(len(js))
+        ]
 
     def far_stage(part, across):
         first = 2 * depth + across * depth
         wires_in(part, 2 + across).wait_recv()
-        values = [values_of(part, first + ahead) for ahead in range(depth)]
+        values = values_of(part, range(first, first + depth))
         for ahead, value in enumerate(values):
             core_out[across, ahead, span(part)] = value
         core_copy(part, across).start()
 
     def side_stage(part):
         wires_in(part, 1).wait_recv()
-        values = [values_of(part, depth + ahead) for ahead in range(depth)]
+        values = values_of(part, range(depth, 2 * depth))
         core_copy(part, 1).wait_recv()
         for ahead, value in enumerate(values):
             side_out[ahead, span(part)] = (value + core_in[1, ahead, span(part)]).astype(
@@ -667,14 +693,14 @@
 
     def line_stage(part):
         wires_in(part, 0).wait_recv()
-        values = [values_of(part, ahead) for ahead in range(1, depth)]
+        values = values_of(part, range(1, depth))
         core_copy(part, 0).wait_recv()
         side_copy(part).wait_recv()
         for ahead in range(1, depth):
             value = values[ahead - 1] + core_in[0, ahead, span(part)]
             value = value + side_in[ahead, span(part)].astype(jnp.float32)
             line_out[ahead, span(part)] = value.astype(jnp.bfloat16)
-        for ahead in range(1, depth):
+        for ahead in reversed(range(1, depth)):
             line_copy(part, ahead).start()
 
     far_stage(0, 1)
@@ -690,9 +716,10 @@
     far_stage(2, 0)
     line_stage(2)
 
-    for part in range(len(parts)):
-        value = values_of(part, 0) + fresh_ref[span(part)] + core_in[0, 0, span(part)]
-        keep_ref[span(part)] = value + side_in[0, span(part)].astype(jnp.float32)
+    own = partials([(unit, 0) for unit in range(units)])
+    keep_ref[...] = (
+        jnp.concatenate(own, 0) + fresh_ref[...] + core_in[0, 0] + side_in[0].astype(jnp.float32)
+    )
     all_asks.wait_send()
     for part in range(len(parts)):
         wires_out(part).wait_send()
@@ -768,7 +795,7 @@
         out_specs=vmem,
         out_shape=pltpu.VMEM((steps, heads * group * HEAD_SIZE), f32),
         scratch_shapes=[
-            pltpu.VMEM((deep, tokens), bf16),
+            pltpu.VMEM((rank, tokens), bf16),
             pltpu.VMEM((rank, heads * HEAD_SIZE), bf16),
             pltpu.VMEM((steps * picks, steps * picks * BLOCK_TOKENS), bf16),
             pltpu.VMEM((lines, 2 * lines), bf16),
@@ -785,7 +812,7 @@
             pltpu.VMEM((steps * heads, group, HEAD_SIZE), bf16),
             pltpu.VMEM((heads, both, 8), f32),
             pltpu.VMEM((heads, 8, HEAD_SIZE), bf16),
-            pltpu.VMEM((heads, deep, 2 * HEAD_SIZE), bf16),
+            pltpu.VMEM((heads, rank, 2 * HEAD_SIZE), bf16),
             pltpu.VMEM((picks * BLOCK_TOKENS, 2 * HEAD_SIZE), f32),
             pltpu.VMEM((picks * BLOCK_TOKENS, 2 * HEAD_SIZE), f32),
             pltpu.VMEM((picks * BLOCK_TOKENS, 2 * HEAD_SIZE), f32),

time: 29.8 us -> 28.9 us (0.970)
  Pallas kernels: 28.3 us -> 27.4 us
    pallas_call x1, Pallas kernels: 28.3 us -> 27.4 us  [fused_device(): pl.pallas_call(functools.partial(fused_kernel, share, pool_here), in_spec...]
where the time goes in v5:
time: 28.9 us; the launch traced here: 28.7 us
  Pallas kernels  27.4 us (95%)
  between operations  0.66 us (2%)
  other arithmetic  0.64 us (2%)
    pallas_call x1, Pallas kernels, fused_device(): pl.pallas_call(functools.partial(fused_kernel, share, pool_here), in_spec...  27.4 us
    reshape x1, other arithmetic, fused_device(): return attended.astype(bf16).reshape(steps, 1, -1)  0.64 us

profile of v5, /device:TPU:0, one launch (start us, length us, event | category | flops | bytes accessed | tf_op | source)
XLA Modules:
  0.0 28.7 jit_solution(159139441504647664)
XLA Ops:
  0.7 27.4 %fused.1 = f32[2,8192]{1,0:T(2,128)S(1)} custom-call(s32[1]{0:T(128)S(6)} %copy.15.length_ref, s32[16,64]{1,0:T(8,128)} %bitcast.16, f32[4,128]{1,0:T(4,128)} %constant.10.clone.ahead_ref, bf16[2,8192]{1,0:T(2,128)(2,1)} %bitcast.15, bf16[2,1024]{1,0:T(2,128)(2,1)} %bitcast.19, bf16[2,1024]{1,0:T(2,128)(2,1)} %bitcast.20, s32[16,64]{1,0:T(8,128)} %bitcast.17, ...), custom_call_target="tpu_custom_call" | custom-call | tf_op jit(solution)/shard_map/fused/pallas_call | solution.py:792
  28.1 0.6 %convert_bitcast_fusion = bf16[2,1,8192]{2,0,1:T(2,128)(2,1)} fusion(f32[2,8192]{1,0:T(2,128)S(1)} %fused.1), kind=kLoop, calls=%fused_computation | loop fusion | flops 16384 | bytes 98304 | tf_op jit(solution)/shard_map/reshape | solution.py:845

commit v6 on v5

--- a/solution.py
+++ b/solution.py
@@ -192,9 +192,9 @@
     send_ref, ask_ref, asked_ref, row_ref, place_ref, sign_ref, bound_ref,
     rotated_ref, fresh_score_ref, fresh_value_ref, factor_ref, raw_even, raw_odd, turn_even, turn_odd, score_ref, fresh_ref,
     routed_ref, wire_ref, got_ref,
-    core_out, core_in, side_out, side_in, line_out, line_in, keep_ref,
+    core_out, core_in, last_out, last_in, keep_ref,
     in_sem, pool_sem, row_sem, ask_send, ask_recv, wire_send, wire_recv,
-    core_send, core_recv, side_send, side_recv, line_send, line_recv,
+    core_send, core_recv, last_send, last_recv,
 ):
     me = lax.axis_index("store")
     raw_refs, turn_refs = (raw_even, raw_odd), (turn_even, turn_odd)
@@ -332,8 +332,10 @@
             send_ref.at[target], ask_ref.at[j], ask_send.at[0], ask_recv.at[0], target
         )
 
+    turn_of = (3, 2, 1, 0)
     far_first = sorted(
-        range(1, holders), key=lambda j: (-(min(j % depth, depth - j % depth)), -j)
+        range(1, holders),
+        key=lambda j: (turn_of[j // depth], -min(j % depth, depth - j % depth)),
     )
     pl.semaphore_wait(barrier, holders - 1)
     for j in far_first:
@@ -357,10 +359,13 @@
     loads[0].wait()
     turned_blocks = total // BLOCK_TOKENS
     for at in range(0, left_ref.shape[1], total):
-        turned = lax.dot_general(
-            same, left_ref[:, at : at + total], (((1,), (1,)), ((), ())),
-            preferred_element_type=jnp.float32,
-        )
+        if at // total % 2 == 1:
+            turned = left_ref[:, at : at + total].astype(jnp.float32).T
+        else:
+            turned = lax.dot_general(
+                same, left_ref[:, at : at + total], (((1,), (1,)), ((), ())),
+                preferred_element_type=jnp.float32,
+            )
         first = at // BLOCK_TOKENS
         block_ref[first : first + turned_blocks, :, :rank] = turned.reshape(
             turned_blocks, BLOCK_TOKENS, rank
@@ -562,6 +567,11 @@
                 step *= 2
             for holder in range(holders):
                 wire_ref[holder, unit] = cells[holder].astype(jnp.bfloat16)
+    others = pl.ds(1, holders - 1)
+    all_asks = remote(
+        send_ref.at[others], ask_ref.at[others], ask_send.at[0], ask_recv.at[0], peer(1)
+    )
+    row_copy = pltpu.make_async_copy(asked_ref, row_ref, row_sem.at[0])
     key_rows(0, 2 * parts[0][1] * steps)
     for part, (first, last) in enumerate(parts):
         later = [
@@ -577,18 +587,14 @@
             key_rows(*later.pop(0))
         for j in far_first:
             wire_copy(part, j).start()
+        if part == 1:
+            all_asks.wait_recv()
+            asked_ref[...] = jnp.clip(ask_ref[...], 0, pool_ref.shape[0] - 1)
+            row_copy.start()
         for span_rows in later:
             key_rows(*span_rows)
 
     loads[5].wait()
-    others = pl.ds(1, holders - 1)
-    all_asks = remote(
-        send_ref.at[others], ask_ref.at[others], ask_send.at[0], ask_recv.at[0], peer(1)
-    )
-    all_asks.wait_recv()
-    asked_ref[...] = jnp.clip(ask_ref[...], 0, pool_ref.shape[0] - 1)
-    row_copy = pltpu.make_async_copy(asked_ref, row_ref, row_sem.at[0])
-    row_copy.start()
     row_copy.wait()
     pltpu.make_async_copy(pool_ref, pool_ref, pool_sem.at[0]).wait()
 
@@ -633,7 +639,6 @@
         return jnp.concatenate([product[:both, :HEAD_SIZE], product[both:, HEAD_SIZE:]], 0)
 
     own_core = peer(2 * depth)
-    own_side = peer(depth)
 
     def span(part):
         first, last = parts[part]
@@ -644,25 +649,6 @@
         return remote(
             core_out.at[across, :, span(part)], core_in.at[across, :, span(part)],
             core_send.at[at], core_recv.at[at], own_core,
-        )
-
-    def side_copy(part):
-        return remote(
-            side_out.at[:, span(part)], side_in.at[:, span(part)],
-            side_send.at[part], side_recv.at[part], own_side,
-        )
-
-    def line_copy(part, ahead):
-        return remote(
-            line_out.at[ahead, span(part)], line_in.at[ahead, span(part)],
-            line_send.at[part], line_recv.at[part],
-            lax.rem(layer - ahead + depth, depth) * 4 + side * 2 + core,
-        )
-
-    def all_lines(part):
-        rest = (pl.ds(1, depth - 1), span(part))
-        return remote(
-            line_out.at[rest], line_in.at[rest], line_send.at[part], line_recv.at[part], peer(1)
         )
 
     def values_of(part, js):
@@ -681,70 +667,66 @@
             core_out[across, ahead, span(part)] = value
         core_copy(part, across).start()
 
-    def side_stage(part):
+    def direct_copy(part, slot):
+        across, ahead = slot // depth, slot % depth
+        return remote(
+            last_out.at[slot, span(part)], last_in.at[slot, span(part)],
+            last_send.at[part], last_recv.at[part],
+            lax.rem(layer - ahead + depth, depth) * 4
+            + (1 - side if across else side) * 2 + core,
+        )
+
+    def all_direct(part):
+        every = (pl.ds(1, 2 * depth - 1), span(part))
+        return remote(
+            last_out.at[every], last_in.at[every], last_send.at[part], last_recv.at[part], peer(1)
+        )
+
+    def near_stage(part):
         wires_in(part, 1).wait_recv()
-        values = values_of(part, range(depth, 2 * depth))
+        wires_in(part, 0).wait_recv()
+        values = values_of(part, range(1, 2 * depth))
         core_copy(part, 1).wait_recv()
-        for ahead, value in enumerate(values):
-            side_out[ahead, span(part)] = (value + core_in[1, ahead, span(part)]).astype(
-                jnp.bfloat16
-            )
-        side_copy(part).start()
-
-    def line_stage(part):
-        wires_in(part, 0).wait_recv()
-        values = values_of(part, range(1, depth))
         core_copy(part, 0).wait_recv()
-        side_copy(part).wait_recv()
-        for ahead in range(1, depth):
-            value = values[ahead - 1] + core_in[0, ahead, span(part)]
-            value = value + side_in[ahead, span(part)].astype(jnp.float32)
-            line_out[ahead, span(part)] = value.astype(jnp.bfloat16)
-        for ahead in reversed(range(1, depth)):
-            line_copy(part, ahead).start()
-
-    far_stage(0, 1)
-    side_stage(0)
-    far_stage(1, 1)
-    side_stage(1)
-    far_stage(0, 0)
-    far_stage(2, 1)
-    side_stage(2)
-    line_stage(0)
-    far_stage(1, 0)
-    line_stage(1)
-    far_stage(2, 0)
-    line_stage(2)
-
+        for slot in range(1, 2 * depth):
+            last_out[slot, span(part)] = (
+                values[slot - 1] + core_in[slot // depth, slot % depth, span(part)]
+            ).astype(jnp.bfloat16)
+        for slot in reversed(range(1, 2 * depth)):
+            direct_copy(part, slot).start()
+
+    def finish(part):
+        all_direct(part).wait_recv()
+        value = keep_ref[span(part)]
+        for slot in range(1, 2 * depth):
+            value = value + last_in[slot, span(part)].astype(jnp.float32)
+        keep_ref[span(part)] = value
+        for head in range(2 * parts[part][0], 2 * parts[part][1]):
+            for g in range(group):
+                at = (head * group + g) * HEAD_SIZE
+                out_ref[:, at : at + HEAD_SIZE] = jnp.concatenate(
+                    [
+                        keep_ref[head * both + s * group + g : head * both + s * group + g + 1]
+                        for s in range(steps)
+                    ],
+                    0,
+                )
+
+    for part in range(len(parts)):
+        far_stage(part, 1)
+        far_stage(part, 0)
+        near_stage(part)
     own = partials([(unit, 0) for unit in range(units)])
-    keep_ref[...] = (
-        jnp.concatenate(own, 0) + fresh_ref[...] + core_in[0, 0] + side_in[0].astype(jnp.float32)
-    )
+    keep_ref[...] = jnp.concatenate(own, 0) + fresh_ref[...] + core_in[0, 0]
     all_asks.wait_send()
     for part in range(len(parts)):
         wires_out(part).wait_send()
         core_copy(part, 0).wait_send()
         core_copy(part, 1).wait_send()
-        side_copy(part).wait_send()
     for part in range(len(parts)):
-        all_lines(part).wait_recv()
-        value = keep_ref[span(part)]
-        for ahead in range(1, depth):
-            value = value + line_in[ahead, span(part)].astype(jnp.float32)
-        keep_ref[span(part)] = value
-    for head in range(heads):
-        for g in range(group):
-            at = (head * group + g) * HEAD_SIZE
-            out_ref[:, at : at + HEAD_SIZE] = jnp.concatenate(
-                [
-                    keep_ref[head * both + s * group + g : head * both + s * group + g + 1]
-                    for s in range(steps)
-                ],
-                0,
-            )
-
+        finish(part)
     for part in range(len(parts)):
-        all_lines(part).wait_send()
+        all_direct(part).wait_send()
 
 
 def fused_device(
@@ -824,13 +806,11 @@
             pltpu.VMEM((holders, units, both, lines), bf16),
             pltpu.VMEM((2, depth, rows, HEAD_SIZE), f32),
             pltpu.VMEM((2, depth, rows, HEAD_SIZE), f32),
-            pltpu.VMEM((depth, rows, HEAD_SIZE), bf16),
-            pltpu.VMEM((depth, rows, HEAD_SIZE), bf16),
-            pltpu.VMEM((depth, rows, HEAD_SIZE), bf16),
-            pltpu.VMEM((depth, rows, HEAD_SIZE), bf16),
+            pltpu.VMEM((2 * depth, rows, HEAD_SIZE), bf16),
+            pltpu.VMEM((2 * depth, rows, HEAD_SIZE), bf16),
             pltpu.VMEM((rows, HEAD_SIZE), f32),
             dma((6,)), dma((1,)), dma((1,)), dma((1,)), dma((1,)), dma((3,)), dma((12,)),
-            dma((6,)), dma((6,)), dma((3,)), dma((3,)), dma((3,)), dma((3,)),
+            dma((6,)), dma((6,)), dma((3,)), dma((3,)),
         ],
         compiler_params=pltpu.CompilerParams(collective_id=0, has_side_effects=True),
         name="fused",

time: 28.9 us -> 26.2 us (0.907)
  Pallas kernels: 27.4 us -> 24.7 us
    pallas_call x1, Pallas kernels: 27.4 us -> 24.7 us  [fused_device(): pl.pallas_call(functools.partial(fused_kernel, share, pool_here), in_spec...]
where the time goes in v6:
time: 26.2 us; the launch traced here: 26 us
  Pallas kernels  24.7 us (94%)
  between operations  0.66 us (3%)
  other arithmetic  0.64 us (2%)
    pallas_call x1, Pallas kernels, fused_device(): pl.pallas_call(functools.partial(fused_kernel, share, pool_here), in_spec...  24.7 us
    reshape x1, other arithmetic, fused_device(): return attended.astype(bf16).reshape(steps, 1, -1)  0.64 us

profile of v6, /device:TPU:0, one launch (start us, length us, event | category | flops | bytes accessed | tf_op | source)
XLA Modules:
  0.0 26.0 jit_solution(9825942513947555380)
XLA Ops:
  0.7 24.7 %fused.1 = f32[2,8192]{1,0:T(2,128)S(1)} custom-call(s32[1]{0:T(128)S(6)} %copy.15.length_ref, s32[16,64]{1,0:T(8,128)} %bitcast.16, f32[4,128]{1,0:T(4,128)} %constant.10.clone.ahead_ref, bf16[2,8192]{1,0:T(2,128)(2,1)} %bitcast.15, bf16[2,1024]{1,0:T(2,128)(2,1)} %bitcast.19, bf16[2,1024]{1,0:T(2,128)(2,1)} %bitcast.20, s32[16,64]{1,0:T(8,128)} %bitcast.17, ...), custom_call_target="tpu_custom_call" | custom-call | tf_op jit(solution)/shard_map/fused/pallas_call | solution.py:774
  25.3 0.6 %convert_bitcast_fusion = bf16[2,1,8192]{2,0,1:T(2,128)(2,1)} fusion(f32[2,8192]{1,0:T(2,128)S(1)} %fused.1), kind=kLoop, calls=%fused_computation | loop fusion | flops 16384 | bytes 98304 | tf_op jit(solution)/shard_map/reshape | solution.py:825

commit v7 on v6

--- a/solution.py
+++ b/solution.py
@@ -209,7 +209,7 @@
     both = steps * group
     half = HEAD_SIZE // 2
     units = heads // 2
-    parts = ((0, units - 2), (units - 2, units - 1), (units - 1, units))
+    parts = ((0, units - 2), (units - 2, units))
     scale = HEAD_SIZE ** (-0.5)
     core, side, layer = lax.rem(me, 2), lax.rem(me // 2, 2), me // 4
 
@@ -235,8 +235,6 @@
             device_id_type=pl.DeviceIdType.MESH,
         )
         return 0
-
-    lax.fori_loop(1, holders, greet, 0)
 
     loads = [
         pltpu.make_async_copy(src, dst, in_sem.at[at])
@@ -253,6 +251,8 @@
     ]
     for copy in loads:
         copy.start()
+    lax.fori_loop(1, holders, greet, 0)
+
     octets = pool_here // 8
     pool_copies = [
         pltpu.make_async_copy(
@@ -426,7 +426,7 @@
     ).astype(jnp.float32)
     low_half = lax.broadcasted_iota(jnp.int32, (group, total), 1) < picks
 
-    portion = 2 * total // BLOCK_TOKENS
+    portion = 4 * total // BLOCK_TOKENS
     portions = picks // portion
 
     def gather(row, at):
@@ -434,7 +434,7 @@
         found = [
             block_ref[pick_ref[s * heads + head, at * portion + n]] for n in range(portion)
         ]
-        span = slice(2 * at * total, 2 * (at + 1) * total)
+        span = slice(4 * at * total, 4 * (at + 1) * total)
         raw_refs[row % 2][span] = jnp.dot(
             jnp.concatenate([value[:, :rank] for value in found], 0).astype(jnp.bfloat16),
             factor_ref[head], preferred_element_type=jnp.float32,
@@ -443,7 +443,7 @@
 
     def compare(row, at):
         head, s = divmod(row, steps)
-        span = slice(2 * at * total, 2 * (at + 1) * total)
+        span = slice(4 * at * total, 4 * (at + 1) * total)
         raw = raw_refs[row % 2][span]
         keys = raw * turn_refs[row % 2][span]
         keys = keys[:, :HEAD_SIZE] + keys[:, HEAD_SIZE:]
@@ -575,7 +575,10 @@
     key_rows(0, 2 * parts[0][1] * steps)
     for part, (first, last) in enumerate(parts):
         later = [
-            (row, row + 1) for row in range(2 * last * steps, 2 * (last + 1) * steps) if row < rows
+            (row, row + 1)
+            for row in range(
+                2 * last * steps, 2 * parts[min(part + 1, len(parts) - 1)][1] * steps
+            )
         ]
         for _ in weigh(part):
             if later:
@@ -583,11 +586,9 @@
         if later:
             key_rows(*later.pop(0))
         cross(first, last)
-        if later:
-            key_rows(*later.pop(0))
         for j in far_first:
             wire_copy(part, j).start()
-        if part == 1:
+        if part == 0:
             all_asks.wait_recv()
             asked_ref[...] = jnp.clip(ask_ref[...], 0, pool_ref.shape[0] - 1)
             row_copy.start()

time: 26.2 us -> 25.5 us (0.973)
  Pallas kernels: 24.7 us -> 24 us
    pallas_call x1, Pallas kernels: 24.7 us -> 24 us  [fused_device(): pl.pallas_call(functools.partial(fused_kernel, share, pool_here), in_spec...]
where the time goes in v7:
time: 25.5 us; the launch traced here: 25.3 us
  Pallas kernels  24 us (94%)
  between operations  0.66 us (3%)
  other arithmetic  0.64 us (3%)
    pallas_call x1, Pallas kernels, fused_device(): pl.pallas_call(functools.partial(fused_kernel, share, pool_here), in_spec...  24 us
    reshape x1, other arithmetic, fused_device(): return attended.astype(bf16).reshape(steps, 1, -1)  0.64 us

profile of v7, /device:TPU:0, one launch (start us, length us, event | category | flops | bytes accessed | tf_op | source)
XLA Modules:
  0.0 25.3 jit_solution(8767198554218428220)
XLA Ops:
  0.7 24.0 %fused.1 = f32[2,8192]{1,0:T(2,128)S(1)} custom-call(s32[1]{0:T(128)S(6)} %copy.15.length_ref, s32[16,64]{1,0:T(8,128)} %bitcast.16, f32[4,128]{1,0:T(4,128)} %constant.10.clone.ahead_ref, bf16[2,8192]{1,0:T(2,128)(2,1)} %bitcast.15, bf16[2,1024]{1,0:T(2,128)(2,1)} %bitcast.19, bf16[2,1024]{1,0:T(2,128)(2,1)} %bitcast.20, s32[16,64]{1,0:T(8,128)} %bitcast.17, ...), custom_call_target="tpu_custom_call" | custom-call | tf_op jit(solution)/shard_map/fused/pallas_call | solution.py:775
  24.7 0.6 %convert_bitcast_fusion = bf16[2,1,8192]{2,0,1:T(2,128)(2,1)} fusion(f32[2,8192]{1,0:T(2,128)S(1)} %fused.1), kind=kLoop, calls=%fused_computation | loop fusion | flops 16384 | bytes 98304 | tf_op jit(solution)/shard_map/reshape | solution.py:826

commit v8 on v7

--- a/solution.py
+++ b/solution.py
@@ -359,7 +359,7 @@
     loads[0].wait()
     turned_blocks = total // BLOCK_TOKENS
     for at in range(0, left_ref.shape[1], total):
-        if at // total % 2 == 1:
+        if at // total % 3 != 0:
             turned = left_ref[:, at : at + total].astype(jnp.float32).T
         else:
             turned = lax.dot_general(
@@ -683,17 +683,16 @@
             last_out.at[every], last_in.at[every], last_send.at[part], last_recv.at[part], peer(1)
         )
 
-    def near_stage(part):
-        wires_in(part, 1).wait_recv()
-        wires_in(part, 0).wait_recv()
-        values = values_of(part, range(1, 2 * depth))
-        core_copy(part, 1).wait_recv()
-        core_copy(part, 0).wait_recv()
-        for slot in range(1, 2 * depth):
+    def near_stage(part, across):
+        wires_in(part, across).wait_recv()
+        slots = range(max(1, across * depth), (across + 1) * depth)
+        values = values_of(part, slots)
+        core_copy(part, across).wait_recv()
+        for slot, value in zip(slots, values):
             last_out[slot, span(part)] = (
-                values[slot - 1] + core_in[slot // depth, slot % depth, span(part)]
+                value + core_in[across, slot % depth, span(part)]
             ).astype(jnp.bfloat16)
-        for slot in reversed(range(1, 2 * depth)):
+        for slot in reversed(slots):
             direct_copy(part, slot).start()
 
     def finish(part):
@@ -716,8 +715,10 @@
     for part in range(len(parts)):
         far_stage(part, 1)
         far_stage(part, 0)
-        near_stage(part)
-    own = partials([(unit, 0) for unit in range(units)])
+        near_stage(part, 1)
+        near_stage(part, 0)
+        if part == 0:
+            own = partials([(unit, 0) for unit in range(units)])
     keep_ref[...] = jnp.concatenate(own, 0) + fresh_ref[...] + core_in[0, 0]
     all_asks.wait_send()
     for part in range(len(parts)):

time: 25.5 us -> 25.1 us (0.984)
  Pallas kernels: 24 us -> 23.6 us
    pallas_call x1, Pallas kernels: 24 us -> 23.6 us  [fused_device(): pl.pallas_call(functools.partial(fused_kernel, share, pool_here), in_spec...]
where the time goes in v8:
time: 25.1 us; the launch traced here: 24.9 us
  Pallas kernels  23.6 us (94%)
  between operations  0.66 us (3%)
  other arithmetic  0.64 us (3%)
    pallas_call x1, Pallas kernels, fused_device(): pl.pallas_call(functools.partial(fused_kernel, share, pool_here), in_spec...  23.6 us
    reshape x1, other arithmetic, fused_device(): return attended.astype(bf16).reshape(steps, 1, -1)  0.64 us

profile of v8, /device:TPU:0, one launch (start us, length us, event | category | flops | bytes accessed | tf_op | source)
XLA Modules:
  0.0 24.9 jit_solution(9887877972311883078)
XLA Ops:
  0.7 23.6 %fused.1 = f32[2,8192]{1,0:T(2,128)S(1)} custom-call(s32[1]{0:T(128)S(6)} %copy.15.length_ref, s32[16,64]{1,0:T(8,128)} %bitcast.16, f32[4,128]{1,0:T(4,128)} %constant.10.clone.ahead_ref, bf16[2,8192]{1,0:T(2,128)(2,1)} %bitcast.15, bf16[2,1024]{1,0:T(2,128)(2,1)} %bitcast.19, bf16[2,1024]{1,0:T(2,128)(2,1)} %bitcast.20, s32[16,64]{1,0:T(8,128)} %bitcast.17, ...), custom_call_target="tpu_custom_call" | custom-call | tf_op jit(solution)/shard_map/fused/pallas_call | solution.py:776
  24.3 0.6 %convert_bitcast_fusion = bf16[2,1,8192]{2,0,1:T(2,128)(2,1)} fusion(f32[2,8192]{1,0:T(2,128)S(1)} %fused.1), kind=kLoop, calls=%fused_computation | loop fusion | flops 16384 | bytes 98304 | tf_op jit(solution)/shard_map/reshape | solution.py:827
